TPU v7x, 256 devices: a whole 4x4x8 slice. The times are simulated.
256 devices in a mesh: tm: 64 (over z_hi, y, x), chan: 4 (over z_lo, core).
Axes of the slice: x: 4, y: 4, z: 8 (z_hi: 4, z_lo: 2; z = z_hi * 2 + z_lo), core: 2. Of those that a mesh axis runs over, the one named last changes fastest.
Arguments:
- record: bfloat16 [2048, 32768], P('chan', 'tm')
- event_stretch: int32 [4, 2], replicated, may hold values from 0 to 63
- event_offset: int32 [4, 2], replicated, may hold values from 0 to 12
Outputs:
- scores: float32 [4, 2, 32768], P(None, None, 'tm')
Inputs may be any that keep to these rules, and one draw needn't show every extreme that they name: A template lies inside one stretch: event_offset + 500 <= 512.
All inputs are finite; a program needn't handle non-finite values.
Results may differ from a plain program's by a relative error of at most 0.0003.
Values may be sent and summed in bfloat16 or wider, within the bound.
A program may use at most 64 MiB of HBM per device.

v0:
```python
import jax
import jax.numpy as jnp
from jax import lax
from jax.sharding import Mesh
from jax.sharding import PartitionSpec as P

TAPS = 500
STEPS = 4
TM = ("tm_0", "tm_1", "tm_2")


def shifted(x, axis, by):
    peers = lax.axis_size(axis)
    pairs = [(i, i + by) for i in range(peers) if 0 <= i + by < peers]
    return lax.ppermute(x, axis, pairs)


def copy_for_each(x, axis):
    peers = lax.axis_size(axis)
    return lax.all_to_all(jnp.broadcast_to(x[None], (peers, *x.shape)), axis, 0, 0, tiled=True)


def taken_together(x, axis):
    everything = copy_for_each(x, axis)
    return jnp.sum(everything, axis=0)


def filled_up(lines, peers):
    spare = -len(lines) % peers
    return jnp.pad(lines, [(0, spare)] + [(0, 0)] * (lines.ndim - 1))


def laid_out(blocks, dim):
    blocks = jnp.moveaxis(blocks, 0, dim)
    lengths = blocks.shape
    return blocks.reshape(*lengths[:dim], lengths[dim] * lengths[dim + 1], *lengths[dim + 2 :])


def gathered_by_axis(x, axes, dim):
    far, near = axes
    blocks = copy_for_each(copy_for_each(x, far), near)
    return laid_out(blocks.swapaxes(0, 1).reshape(-1, *x.shape), dim)


def cut_along(x, dim, peers):
    lengths = x.shape
    blocks = x.reshape(*lengths[:dim], peers, lengths[dim] // peers, *lengths[dim + 1 :])
    return jnp.moveaxis(blocks, dim, 0)


def sum_at_owner(x, axis, dim):
    peers = lax.axis_size(axis)
    blocks = lax.all_to_all(cut_along(x, dim, peers), axis, 0, 0, tiled=True)
    return jnp.sum(blocks, axis=0)


def sum_in_two_steps(x, axes, dim):
    far, near = axes
    blocks = cut_along(x, dim, lax.axis_size(far))
    nearer = sum_at_owner(blocks, near, dim + 1)
    arrived = lax.all_to_all(nearer, far, split_axis=0, concat_axis=0, tiled=True)
    return arrived.sum(axis=0)


def sum_by_parts(x, axes):
    lines = x.reshape(-1, x.shape[-1])
    padded = filled_up(lines, lax.axis_size(axes[0]) * lax.axis_size(axes[1]))
    whole = gathered_by_axis(sum_in_two_steps(padded, axes, 0), axes, 0)
    return lax.slice_in_dim(whole, 0, len(lines)).reshape(x.shape)


def together(arrays, axis):
    flat, at, finished = (jnp.concatenate([a.reshape(-1) for a in arrays]), 0, [])
    subtotal = taken_together(flat, axis)
    for a in arrays:
        finished.append(subtotal[at : at + a.size].reshape(a.shape))
        at += a.size
    return tuple(finished)


def slide(power, taps, span):
    total = jnp.concatenate([jnp.zeros((1,), jnp.float32), jnp.cumsum(power)])
    return total[taps : taps + span] - total[:span]


def diagonal(product, span):
    count, taps, width = product.shape
    flat = product.reshape(count, taps * width)
    flat = jnp.pad(flat, ((0, 0), (0, taps)))
    return flat.reshape(count, taps, width + 1)[:, :, :span].sum(1)


def local(record, event_stretch, event_offset):
    span = record.shape[1]
    here = lax.axis_index(TM)
    after = shifted(record[:, : TAPS - 1], TM, -1)
    extended = jnp.concatenate([record, after], axis=1)
    wide_ext = extended.astype(jnp.float32)
    power = taken_together(jnp.sum(wide_ext * wide_ext, axis=0), "chan")
    energy = slide(power, TAPS, span)
    results = []
    for step in range(STEPS):
        step_list = [step]
        masked = []
        for fetch_step in step_list:
            for fetch_which in range(2):
                owned = event_stretch[fetch_step, fetch_which] == here
                masked.append(
                    jnp.where(
                        owned,
                        lax.dynamic_slice_in_dim(
                            record, event_offset[fetch_step, fetch_which], TAPS, 1
                        ).astype(jnp.float32),
                        0.0,
                    )
                )
        stacked = jnp.stack(masked).reshape(len(step_list), 2, record.shape[0], TAPS)
        template = sum_by_parts(stacked, (("tm_0", "tm_1"), "tm_2")).astype(jnp.bfloat16)[0]
        wide_tmpl = template.astype(jnp.float32)
        norm_local = jnp.sum(wide_tmpl * wide_tmpl, axis=(1, 2))
        product = jnp.einsum("jck,cr->jkr", template, extended, preferred_element_type=jnp.float32)
        corr_local = diagonal(product, span)
        corr, norms = together((corr_local, norm_local), "chan")
        results.append(corr / jnp.sqrt(energy[None, :] * norms[:, None] + 1e-06))
    return jnp.stack(results)


def solution(mesh):
    torus = Mesh(
        mesh.devices.reshape(4, 4, 4, mesh.shape["chan"]), ("tm_0", "tm_1", "tm_2", "chan")
    )
    return jax.shard_map(
        local,
        mesh=torus,
        in_specs=(P("chan", TM), P(), P()),
        out_specs=P(None, None, TM),
        check_vma=False,
    )
```

profile of v0, /device:TPU:1, one launch (start us, length us, event | category | flops | bytes accessed | tf_op | source)
XLA Modules:
  0.0 526.3 jit_solution(14725839832956945112)
XLA Ops:
  30.9 6.4 %all-to-all-start.5 = ((f32[4,1,1011]{2,1,0:T(1,128)}), f32[4,1,1011]{2,1,0:T(1,128)S(1)}, u32[]{:S(2)}, u32[]{:S(2)}) async-start(f32[4,1,1011]{2,1,0:T(1,128)} %broadcast_in_dim.41), calls=%async_computation.5 | async-start | bytes 32768 | tf_op jit(solution)/shard_map/all_to_all | solution.py:20
  50.6 23.2 %all-to-all-done.6 = f32[4,16,16,500]{3,2,1,0:T(8,128)} async-done(((f32[4,16,16,500]{3,2,1,0:T(8,128)}), f32[4,16,16,500]{3,2,1,0:T(8,128)}, u32[]{:S(2)}, u32[]{:S(2)}) %all-to-all-start.6) | async-done | bytes 2048032 | tf_op jit(solution)/shard_map/all_to_all | solution.py:53
  83.6 20.3 %all-to-all-done = f32[4,16,16,500]{3,2,1,0:T(8,128)} async-done(((f32[4,16,16,500]{3,2,1,0:T(8,128)}), f32[4,16,16,500]{3,2,1,0:T(8,128)}, u32[]{:S(2)}, u32[]{:S(2)}) %all-to-all-start) | async-done | bytes 2048032 | tf_op jit(solution)/shard_map/all_to_all | solution.py:53
  111.7 21.4 %all-to-all-done.16 = f32[4,16,16,500]{3,2,1,0:T(8,128)} async-done(((f32[4,16,16,500]{3,2,1,0:T(8,128)}), f32[4,16,16,500]{3,2,1,0:T(8,128)}, u32[]{:S(2)}, u32[]{:S(2)}) %all-to-all-start.16) | async-done | bytes 2048032 | tf_op jit(solution)/shard_map/all_to_all | solution.py:53
  140.3 21.2 %all-to-all-done.11 = f32[4,16,16,500]{3,2,1,0:T(8,128)} async-done(((f32[4,16,16,500]{3,2,1,0:T(8,128)}), f32[4,16,16,500]{3,2,1,0:T(8,128)}, u32[]{:S(2)}, u32[]{:S(2)}) %all-to-all-start.11) | async-done | bytes 2048032 | tf_op jit(solution)/shard_map/all_to_all | solution.py:53
  161.4 12.6 %all-to-all-start.7 = ((f32[16,16,500]{2,1,0:T(8,128)}), f32[16,16,500]{2,1,0:T(8,128)S(1)}, u32[]{:S(2)}, u32[]{:S(2)}) async-start(f32[16,16,500]{2,1,0:T(8,128)} %reduce_sum.235), calls=%async_computation.7 | async-start | bytes 1048576 | tf_op jit(solution)/shard_map/all_to_all | solution.py:61
  176.7 10.7 %all-to-all-done.7 = f32[16,16,500]{2,1,0:T(8,128)S(1)} async-done(((f32[16,16,500]{2,1,0:T(8,128)}), f32[16,16,500]{2,1,0:T(8,128)S(1)}, u32[]{:S(2)}, u32[]{:S(2)}) %all-to-all-start.7) | async-done | bytes 512032 | tf_op jit(solution)/shard_map/all_to_all | solution.py:61
  187.4 8.6 %all-to-all-start.1 = ((f32[16,16,500]{2,1,0:T(8,128)}), f32[16,16,500]{2,1,0:T(8,128)S(1)}, u32[]{:S(2)}, u32[]{:S(2)}) async-start(f32[16,16,500]{2,1,0:T(8,128)} %reduce_sum.226), calls=%async_computation.1 | async-start | bytes 1048576 | tf_op jit(solution)/shard_map/all_to_all | solution.py:61
  198.7 10.2 %all-to-all-done.1 = f32[16,16,500]{2,1,0:T(8,128)S(1)} async-done(((f32[16,16,500]{2,1,0:T(8,128)}), f32[16,16,500]{2,1,0:T(8,128)S(1)}, u32[]{:S(2)}, u32[]{:S(2)}) %all-to-all-start.1) | async-done | bytes 512032 | tf_op jit(solution)/shard_map/all_to_all | solution.py:61
  208.9 7.5 %all-to-all-start.17 = ((f32[16,16,500]{2,1,0:T(8,128)}), f32[16,16,500]{2,1,0:T(8,128)S(1)}, u32[]{:S(2)}, u32[]{:S(2)}) async-start(f32[16,16,500]{2,1,0:T(8,128)} %reduce_sum.249), calls=%async_computation.17 | async-start | bytes 1048576 | tf_op jit(solution)/shard_map/all_to_all | solution.py:61
  219.1 9.2 %all-to-all-done.17 = f32[16,16,500]{2,1,0:T(8,128)S(1)} async-done(((f32[16,16,500]{2,1,0:T(8,128)}), f32[16,16,500]{2,1,0:T(8,128)S(1)}, u32[]{:S(2)}, u32[]{:S(2)}) %all-to-all-start.17) | async-done | bytes 512032 | tf_op jit(solution)/shard_map/all_to_all | solution.py:61
  228.3 6.3 %all-to-all-start.12 = ((f32[16,16,500]{2,1,0:T(8,128)}), f32[16,16,500]{2,1,0:T(8,128)S(1)}, u32[]{:S(2)}, u32[]{:S(2)}) async-start(f32[16,16,500]{2,1,0:T(8,128)} %reduce_sum.242), calls=%async_computation.12 | async-start | bytes 1048576 | tf_op jit(solution)/shard_map/all_to_all | solution.py:61
  234.7 11.3 %all-to-all-done.12 = f32[16,16,500]{2,1,0:T(8,128)S(1)} async-done(((f32[16,16,500]{2,1,0:T(8,128)}), f32[16,16,500]{2,1,0:T(8,128)S(1)}, u32[]{:S(2)}, u32[]{:S(2)}) %all-to-all-start.12) | async-done | bytes 512032 | tf_op jit(solution)/shard_map/all_to_all | solution.py:61
  250.4 9.9 %all-to-all-done.2 = bf16[16,16,500]{2,1,0:T(8,128)(2,1)S(1)} async-done(((bf16[16,16,500]{2,1,0:T(8,128)(2,1)}), bf16[16,16,500]{2,1,0:T(8,128)(2,1)S(1)}, u32[]{:S(2)}, u32[]{:S(2)}) %all-to-all-start.2) | async-done | bytes 256032 | tf_op jit(solution)/shard_map/all_to_all | solution.py:20
  264.6 9.8 %all-to-all-done.8 = bf16[16,16,500]{2,1,0:T(8,128)(2,1)S(1)} async-done(((bf16[16,16,500]{2,1,0:T(8,128)(2,1)}), bf16[16,16,500]{2,1,0:T(8,128)(2,1)S(1)}, u32[]{:S(2)}, u32[]{:S(2)}) %all-to-all-start.8) | async-done | bytes 256032 | tf_op jit(solution)/shard_map/all_to_all | solution.py:20
  278.8 10.9 %all-to-all-done.13 = bf16[16,16,500]{2,1,0:T(8,128)(2,1)S(1)} async-done(((bf16[16,16,500]{2,1,0:T(8,128)(2,1)}), bf16[16,16,500]{2,1,0:T(8,128)(2,1)S(1)}, u32[]{:S(2)}, u32[]{:S(2)}) %all-to-all-start.13) | async-done | bytes 256032 | tf_op jit(solution)/shard_map/all_to_all | solution.py:20
  289.7 13.7 %all_to_all.110 = bf16[16,16,500]{2,1,0:T(8,128)(2,1)S(1)} all-to-all(bf16[16,16,500]{2,1,0:T(8,128)(2,1)S(1)} %broadcast_in_dim.48), channel_id=1, replica_groups=mesh['tm_0'=4,'tm_1'=4,'tm_2'=4,'chan'=4] {'tm_0','tm_1'}, dimensions={0} | all-to-all | bytes 512000 | tf_op jit(solution)/shard_map/all_to_all | solution.py:20
  303.5 13.1 %all_to_all.111 = bf16[4,16,16,500]{3,2,1,0:T(8,128)(2,1)} all-to-all(bf16[4,16,16,500]{3,2,1,0:T(8,128)(2,1)S(1)} %broadcast_in_dim.43), channel_id=1, replica_groups=mesh['tm_0'=4,'tm_1'=4,'tm_2'=4,'chan'=4] {'tm_2'}, dimensions={0} | all-to-all | bytes 2048000 | tf_op jit(solution)/shard_map/all_to_all | solution.py:20
  321.8 12.1 %all-to-all-done.3 = bf16[4,16,16,500]{3,2,1,0:T(8,128)(2,1)S(1)} async-done(((bf16[4,16,16,500]{3,2,1,0:T(8,128)(2,1)}), bf16[4,16,16,500]{3,2,1,0:T(8,128)(2,1)S(1)}, u32[]{:S(2)}, u32[]{:S(2)}) %all-to-all-start.3) | async-done | bytes 1024032 | tf_op jit(solution)/shard_map/all_to_all | solution.py:20
  349.5 9.5 %reshape.364 = f32[2,505500]{1,0:T(2,128)} reshape(f32[2,500,1011]{2,1,0:T(8,128)} %fusion.4) | data formatting | bytes 8088000 | tf_op jit(solution)/shard_map/reshape | solution.py:88
  359.0 5.8 %pad.18 = f32[2,506000]{1,0:T(2,128)} pad(f32[2,505500]{1,0:T(2,128)} %reshape.364, f32[]{:T(128)} %constant.28.clone.1), padding=0_0x0_500 | pad | bytes 8092004 | tf_op jit(solution)/shard_map/jit(_pad)/pad | solution.py:89
  364.9 9.6 %reshape.365 = f32[2,500,1012]{2,1,0:T(8,128)} reshape(f32[2,506000]{1,0:T(2,128)} %pad.18) | data formatting | bytes 8096000 | tf_op jit(solution)/shard_map/reshape | solution.py:90
  385.3 9.5 %reshape.358 = f32[2,505500]{1,0:T(2,128)} reshape(f32[2,500,1011]{2,1,0:T(8,128)} %fusion.6) | data formatting | bytes 8088000 | tf_op jit(solution)/shard_map/reshape | solution.py:88
  394.8 6.0 %pad.16 = f32[2,506000]{1,0:T(2,128)} pad(f32[2,505500]{1,0:T(2,128)} %reshape.358, f32[]{:T(128)} %constant.28.clone.1), padding=0_0x0_500 | pad | bytes 8092004 | tf_op jit(solution)/shard_map/jit(_pad)/pad | solution.py:89
  400.7 9.6 %reshape.359 = f32[2,500,1012]{2,1,0:T(8,128)} reshape(f32[2,506000]{1,0:T(2,128)} %pad.16) | data formatting | bytes 8096000 | tf_op jit(solution)/shard_map/reshape | solution.py:90
  413.7 25.1 %all-to-all-start.10 = ((f32[4,1,1026]{2,1,0:T(1,128)}), f32[4,1,1026]{2,1,0:T(1,128)S(1)}, u32[]{:S(2)}, u32[]{:S(2)}) async-start(f32[4,1,1026]{2,1,0:T(1,128)} %broadcast_in_dim.44), calls=%async_computation.10 | async-start | bytes 36864 | tf_op jit(solution)/shard_map/all_to_all | solution.py:20
  443.3 9.5 %reshape.372 = f32[2,505500]{1,0:T(2,128)} reshape(f32[2,500,1011]{2,1,0:T(8,128)} %fusion) | data formatting | bytes 8088000 | tf_op jit(solution)/shard_map/reshape | solution.py:88
  452.8 6.1 %pad.20 = f32[2,506000]{1,0:T(2,128)} pad(f32[2,505500]{1,0:T(2,128)} %reshape.372, f32[]{:T(128)} %constant.28.clone.1), padding=0_0x0_500 | pad | bytes 8092004 | tf_op jit(solution)/shard_map/jit(_pad)/pad | solution.py:89
  458.9 9.6 %reshape.373 = f32[2,500,1012]{2,1,0:T(8,128)} reshape(f32[2,506000]{1,0:T(2,128)} %pad.20) | data formatting | bytes 8096000 | tf_op jit(solution)/shard_map/reshape | solution.py:90
  473.5 9.5 %reshape.368 = f32[2,505500]{1,0:T(2,128)} reshape(f32[2,500,1011]{2,1,0:T(8,128)} %fusion.2) | data formatting | bytes 8088000 | tf_op jit(solution)/shard_map/reshape | solution.py:88
  483.0 6.1 %pad.19 = f32[2,506000]{1,0:T(2,128)} pad(f32[2,505500]{1,0:T(2,128)} %reshape.368, f32[]{:T(128)} %constant.28.clone.1), padding=0_0x0_500 | pad | bytes 8092004 | tf_op jit(solution)/shard_map/jit(_pad)/pad | solution.py:89
  489.1 9.6 %reshape.369 = f32[2,500,1012]{2,1,0:T(8,128)} reshape(f32[2,506000]{1,0:T(2,128)} %pad.19) | data formatting | bytes 8096000 | tf_op jit(solution)/shard_map/reshape | solution.py:90
  (124 shorter events, 141.9 us)
Async XLA Ops:
  0.0 24.9 %copy-start = (bf16[512,512]{1,0:T(8,128)(2,1)S(1)}, bf16[512,512]{1,0:T(8,128)(2,1)}, u32[]{:S(2)}) copy-start(bf16[512,512]{1,0:T(8,128)(2,1)} %param.3) | copy-start | bytes 1572868
  0.0 14.2 %copy-start.4 = (s32[4,2]{0,1:T(2,128)S(1)}, s32[4,2]{0,1:T(2,128)}, u32[]{:S(2)}) copy-start(s32[4,2]{0,1:T(2,128)} %param.4) | copy-start | bytes 100
  1.4 28.6 %collective-permute-start = (bf16[512,499]{0,1:T(8,128)(2,1)S(1)}, bf16[512,499]{0,1:T(8,128)(2,1)S(1)}, u32[]{:S(2)}, u32[]{:S(2)}) collective-permute-start(bf16[512,499]{0,1:T(8,128)(2,1)S(1)} %slice.138), channel_id=1, source_target_pairs={{4,0},{8,4},{12,8},{16,12},{20,16},{24,20},{28,24},{32,28},{36,32}... | collective-permute-start | bytes 1532936 | tf_op jit(solution)/shard_map/ppermute | solution.py:15
  30.9 12.1 %all-to-all-start.5 = ((f32[4,1,1011]{2,1,0:T(1,128)}), f32[4,1,1011]{2,1,0:T(1,128)S(1)}, u32[]{:S(2)}, u32[]{:S(2)}) async-start(f32[4,1,1011]{2,1,0:T(1,128)} %broadcast_in_dim.41), calls=%async_computation.5 | async-start | bytes 32768 | tf_op jit(solution)/shard_map/all_to_all | solution.py:20
  43.0 30.9 %all-to-all-start.6 = ((f32[4,16,16,500]{3,2,1,0:T(8,128)}), f32[4,16,16,500]{3,2,1,0:T(8,128)}, u32[]{:S(2)}, u32[]{:S(2)}) async-start(f32[4,16,16,500]{3,2,1,0:T(8,128)} %copy.57), calls=%async_computation.6 | async-start | bytes 4194304 | tf_op jit(solution)/shard_map/all_to_all | solution.py:53
  73.9 30.0 %all-to-all-start = ((f32[4,16,16,500]{3,2,1,0:T(8,128)}), f32[4,16,16,500]{3,2,1,0:T(8,128)}, u32[]{:S(2)}, u32[]{:S(2)}) async-start(f32[4,16,16,500]{3,2,1,0:T(8,128)} %copy.50), calls=%async_computation | async-start | bytes 4194304 | tf_op jit(solution)/shard_map/all_to_all | solution.py:53
  103.9 29.2 %all-to-all-start.16 = ((f32[4,16,16,500]{3,2,1,0:T(8,128)}), f32[4,16,16,500]{3,2,1,0:T(8,128)}, u32[]{:S(2)}, u32[]{:S(2)}) async-start(f32[4,16,16,500]{3,2,1,0:T(8,128)} %copy.65), calls=%async_computation.16 | async-start | bytes 4194304 | tf_op jit(solution)/shard_map/all_to_all | solution.py:53
  133.1 28.3 %all-to-all-start.11 = ((f32[4,16,16,500]{3,2,1,0:T(8,128)}), f32[4,16,16,500]{3,2,1,0:T(8,128)}, u32[]{:S(2)}, u32[]{:S(2)}) async-start(f32[4,16,16,500]{3,2,1,0:T(8,128)} %copy.61), calls=%async_computation.11 | async-start | bytes 4194304 | tf_op jit(solution)/shard_map/all_to_all | solution.py:53
  161.4 26.0 %all-to-all-start.7 = ((f32[16,16,500]{2,1,0:T(8,128)}), f32[16,16,500]{2,1,0:T(8,128)S(1)}, u32[]{:S(2)}, u32[]{:S(2)}) async-start(f32[16,16,500]{2,1,0:T(8,128)} %reduce_sum.235), calls=%async_computation.7 | async-start | bytes 1048576 | tf_op jit(solution)/shard_map/all_to_all | solution.py:61
  187.4 21.5 %all-to-all-start.1 = ((f32[16,16,500]{2,1,0:T(8,128)}), f32[16,16,500]{2,1,0:T(8,128)S(1)}, u32[]{:S(2)}, u32[]{:S(2)}) async-start(f32[16,16,500]{2,1,0:T(8,128)} %reduce_sum.226), calls=%async_computation.1 | async-start | bytes 1048576 | tf_op jit(solution)/shard_map/all_to_all | solution.py:61
  208.9 19.3 %all-to-all-start.17 = ((f32[16,16,500]{2,1,0:T(8,128)}), f32[16,16,500]{2,1,0:T(8,128)S(1)}, u32[]{:S(2)}, u32[]{:S(2)}) async-start(f32[16,16,500]{2,1,0:T(8,128)} %reduce_sum.249), calls=%async_computation.17 | async-start | bytes 1048576 | tf_op jit(solution)/shard_map/all_to_all | solution.py:61
  228.3 17.7 %all-to-all-start.12 = ((f32[16,16,500]{2,1,0:T(8,128)}), f32[16,16,500]{2,1,0:T(8,128)S(1)}, u32[]{:S(2)}, u32[]{:S(2)}) async-start(f32[16,16,500]{2,1,0:T(8,128)} %reduce_sum.242), calls=%async_computation.12 | async-start | bytes 1048576 | tf_op jit(solution)/shard_map/all_to_all | solution.py:61
  246.7 13.6 %all-to-all-start.2 = ((bf16[16,16,500]{2,1,0:T(8,128)(2,1)}), bf16[16,16,500]{2,1,0:T(8,128)(2,1)S(1)}, u32[]{:S(2)}, u32[]{:S(2)}) async-start(bf16[16,16,500]{2,1,0:T(8,128)(2,1)} %broadcast_in_dim.38), calls=%async_computation.2 | async-start | bytes 524288 | tf_op jit(solution)/shard_map/all_to_all | solution.py:20
  261.1 13.4 %all-to-all-start.8 = ((bf16[16,16,500]{2,1,0:T(8,128)(2,1)}), bf16[16,16,500]{2,1,0:T(8,128)(2,1)S(1)}, u32[]{:S(2)}, u32[]{:S(2)}) async-start(bf16[16,16,500]{2,1,0:T(8,128)(2,1)} %broadcast_in_dim.42), calls=%async_computation.8 | async-start | bytes 524288 | tf_op jit(solution)/shard_map/all_to_all | solution.py:20
  275.2 14.5 %all-to-all-start.13 = ((bf16[16,16,500]{2,1,0:T(8,128)(2,1)}), bf16[16,16,500]{2,1,0:T(8,128)(2,1)S(1)}, u32[]{:S(2)}, u32[]{:S(2)}) async-start(bf16[16,16,500]{2,1,0:T(8,128)(2,1)} %broadcast_in_dim.45), calls=%async_computation.13 | async-start | bytes 524288 | tf_op jit(solution)/shard_map/all_to_all | solution.py:20
  317.7 16.3 %all-to-all-start.3 = ((bf16[4,16,16,500]{3,2,1,0:T(8,128)(2,1)}), bf16[4,16,16,500]{3,2,1,0:T(8,128)(2,1)S(1)}, u32[]{:S(2)}, u32[]{:S(2)}) async-start(bf16[4,16,16,500]{3,2,1,0:T(8,128)(2,1)} %broadcast_in_dim.39), calls=%async_computation.3 | async-start | bytes 2097152 | tf_op jit(solution)/shard_map/all_to_all | solution.py:20
  334.0 1.4 copy-start.1
  335.4 39.1 %all-to-all-start.14 = ((bf16[4,16,16,500]{3,2,1,0:T(8,128)(2,1)}), bf16[4,16,16,500]{3,2,1,0:T(8,128)(2,1)S(1)}, u32[]{:S(2)}, u32[]{:S(2)}) async-start(bf16[4,16,16,500]{3,2,1,0:T(8,128)(2,1)} %broadcast_in_dim.46), calls=%async_computation.14 | async-start | bytes 2097152 | tf_op jit(solution)/shard_map/all_to_all | solution.py:20
  375.5 37.6 %all-to-all-start.19 = ((bf16[4,16,16,500]{3,2,1,0:T(8,128)(2,1)}), bf16[4,16,16,500]{3,2,1,0:T(8,128)(2,1)}, u32[]{:S(2)}, u32[]{:S(2)}) async-start(bf16[4,16,16,500]{3,2,1,0:T(8,128)(2,1)} %broadcast_in_dim.49), calls=%async_computation.19 | async-start | bytes 2097152 | tf_op jit(solution)/shard_map/all_to_all | solution.py:20
  380.2 1.8 copy-start.3
  413.7 88.8 %all-to-all-start.10 = ((f32[4,1,1026]{2,1,0:T(1,128)}), f32[4,1,1026]{2,1,0:T(1,128)S(1)}, u32[]{:S(2)}, u32[]{:S(2)}) async-start(f32[4,1,1026]{2,1,0:T(1,128)} %broadcast_in_dim.44), calls=%async_computation.10 | async-start | bytes 36864 | tf_op jit(solution)/shard_map/all_to_all | solution.py:20
  468.5 1.8 copy-start.2
  503.1 6.4 %all-to-all-start.4 = ((f32[4,1,1026]{2,1,0:T(1,128)}), f32[4,1,1026]{2,1,0:T(1,128)S(1)}, u32[]{:S(2)}, u32[]{:S(2)}) async-start(f32[4,1,1026]{2,1,0:T(1,128)} %broadcast_in_dim.40), calls=%async_computation.4 | async-start | bytes 36864 | tf_op jit(solution)/shard_map/all_to_all | solution.py:20
  510.2 7.1 %all-to-all-start.20 = ((f32[4,1,1026]{2,1,0:T(1,128)}), f32[4,1,1026]{2,1,0:T(1,128)S(1)}, u32[]{:S(2)}, u32[]{:S(2)}) async-start(f32[4,1,1026]{2,1,0:T(1,128)} %broadcast_in_dim.50), calls=%async_computation.20 | async-start | bytes 36864 | tf_op jit(solution)/shard_map/all_to_all | solution.py:20
  517.9 7.1 %all-to-all-start.15 = ((f32[4,1,1026]{2,1,0:T(1,128)}), f32[4,1,1026]{2,1,0:T(1,128)S(1)}, u32[]{:S(2)}, u32[]{:S(2)}) async-start(f32[4,1,1026]{2,1,0:T(1,128)} %broadcast_in_dim.47), calls=%async_computation.15 | async-start | bytes 36864 | tf_op jit(solution)/shard_map/all_to_all | solution.py:20
where the time goes:
time: 537 us; the launch traced here: 526 us
  waiting for transfers between devices  179 us (33%)
  local copies, waits for them, and re-layouts  129 us (24%)
  starting transfers between devices  119 us (22%)
  other arithmetic  38.3 us (7%)
  blocking collectives  26.7 us (5%)
  between operations  20.8 us (4%)
  matrix products  12.9 us (2%)
    all_to_all x4, waiting for transfers between devices, sum_at_owner(): blocks = lax.all_to_all(cut_along(x, dim, peers), axis, 0, 0, tiled=True)  86.1 us
    all_to_all x11, starting transfers between devices, copy_for_each(): lax.all_to_all(jnp.broadcast_to(x[None], (peers, *x.shape)), axis, 0, 0,...  65.3 us
    all_to_all x11, waiting for transfers between devices, copy_for_each(): lax.all_to_all(jnp.broadcast_to(x[None], (peers, *x.shape)), axis, 0, 0,...  51.7 us
    all_to_all x4, waiting for transfers between devices, sum_in_two_steps(): lax.all_to_all(nearer, far, split_axis=0, concat_axis=0, tiled=True)  41.4 us
    reshape x4, local copies, waits for them, and re-layouts, diagonal(): return flat.reshape(count, taps, width + 1)[:, :, :span].sum(1)  38.2 us
    reshape x4, local copies, waits for them, and re-layouts, diagonal(): flat = product.reshape(count, taps * width)  38 us
    all_to_all x4, starting transfers between devices, sum_in_two_steps(): lax.all_to_all(nearer, far, split_axis=0, concat_axis=0, tiled=True)  35 us
    all_to_all x2, blocking collectives, copy_for_each(): lax.all_to_all(jnp.broadcast_to(x[None], (peers, *x.shape)), axis, 0, 0,...  26.7 us
  transfers between devices with their start and end apart: 20, of which 15 were waited for; matrix products, arithmetic and copies ran while one was open for 32% of the time, Pallas kernels for 0%

commit v1 on v0

v1 whole, which is shorter than its diff:
```python
import functools
import itertools

import jax
import jax.numpy as jnp
from jax import lax
from jax.experimental import pallas as pl
from jax.experimental.pallas import tpu as pltpu
from jax.sharding import Mesh
from jax.sharding import PartitionSpec as P

TAPS = 500
AXES = ("zh", "y", "x", "zl", "core")
SIZE = {"zh": 4, "y": 4, "x": 4, "zl": 2, "core": 2}
MESH = pl.DeviceIdType.MESH
F32 = jnp.float32
BF16 = jnp.bfloat16
SPAN = 512
PLANE = 16
CH = 32
EVENTS = 8
SUB = 32
CHUNK = 2048
WIDE = SPAN + 128


def steps(axes):
    grid = itertools.product(*[range(SIZE[a]) for a in axes])
    return [dict(zip(axes, at)) for at in grid if any(at)]


def moved(me, by, sign=1):
    return {a: lax.rem(me[a] + sign * by[a] + SIZE[a], SIZE[a]) for a in by}


def spot(at, axes):
    index = 0
    for a in axes:
        index = index * SIZE[a] + at[a]
    return index


def remote(src, dst, send, recv, to):
    return pltpu.make_async_remote_copy(
        src_ref=src, dst_ref=dst, send_sem=send, recv_sem=recv, device_id=to, device_id_type=MESH
    )


def greet(me, groups):
    barrier = pltpu.get_barrier_semaphore()
    count = 0
    for axes in groups:
        for by in steps(axes):
            pl.semaphore_signal(barrier, inc=1, device_id=moved(me, by), device_id_type=MESH)
            count += 1
    pl.semaphore_wait(barrier, count)


def exchange_kernel(
    where_ref, x_ref, rec_ref, next_ref, tmpl_ref, cand, picks, s_xy, r_xy, s_z, r_z, s_g, r_g, s_h, r_h, own
):
    me = {a: lax.axis_index(a) for a in AXES}
    greet(me, [("y", "x"), ("zh",)])
    here = spot(me, ("y", "x"))
    zh = me["zh"]
    flat = steps(("y", "x"))
    out = []
    for by in flat:
        to = moved(me, by)
        there = spot(to, ("y", "x"))
        copy = remote(x_ref.at[there], rec_ref.at[here], s_xy.at[there], r_xy.at[here], to)
        copy.start()
        out.append(copy)
    keep = pltpu.make_async_copy(x_ref.at[here], rec_ref.at[here], own)
    keep.start()
    keep.wait()
    for by in flat:
        source = moved(me, by, -1)
        there = spot(source, ("y", "x"))
        remote(x_ref.at[there], rec_ref.at[there], s_xy.at[there], r_xy.at[there], source).wait_recv()

    for j in range(EVENTS):
        cand[j // 2, j % 2] = rec_ref[lax.rem(where_ref[j], PLANE)]
    back = {"zh": lax.rem(zh + 3, 4)}
    for d in (2, 1, 3):
        to = {"zh": lax.rem(zh + d, 4)}
        copy = remote(cand.at[to["zh"]], picks.at[zh], s_z.at[to["zh"]], r_z.at[zh], to)
        copy.start()
        out.append(copy)
    halo = remote(rec_ref.at[0], next_ref, s_h, r_h, back)
    halo.start()
    picks[zh] = cand[zh]
    for d in (1, 2, 3):
        q = lax.rem(zh + d, 4)
        remote(cand.at[q], picks.at[q], s_z.at[q], r_z.at[q], {"zh": q}).wait_recv()

    for i in range(2):
        tmpl_ref[zh, i] = picks[lax.div(where_ref[2 * zh + i], PLANE), i]
    for d in (2, 1, 3):
        to = {"zh": lax.rem(zh + d, 4)}
        copy = remote(tmpl_ref.at[zh], tmpl_ref.at[zh], s_g.at[to["zh"]], r_g.at[zh], to)
        copy.start()
        out.append(copy)
    for d in (1, 2, 3):
        q = lax.rem(zh + d, 4)
        remote(tmpl_ref.at[q], tmpl_ref.at[q], s_g.at[q], r_g.at[q], {"zh": q}).wait_recv()
    halo.wait()
    for copy in out:
        copy.wait_send()


def exchange(where, record):
    dma = pltpu.SemaphoreType.DMA
    return pl.pallas_call(
        exchange_kernel,
        out_shape=(
            jax.ShapeDtypeStruct((PLANE, CH, SPAN), BF16),
            jax.ShapeDtypeStruct((CH, SPAN), BF16),
            jax.ShapeDtypeStruct((4, 2, CH, SPAN), BF16),
        ),
        in_specs=[pl.BlockSpec(memory_space=pltpu.SMEM), pl.BlockSpec(memory_space=pl.ANY)],
        out_specs=(pl.BlockSpec(memory_space=pltpu.VMEM),) * 3,
        scratch_shapes=[
            pltpu.VMEM((4, 2, CH, SPAN), BF16),
            pltpu.VMEM((4, 2, CH, SPAN), BF16),
            dma((PLANE,)),
            dma((PLANE,)),
            dma((4,)),
            dma((4,)),
            dma((4,)),
            dma((4,)),
            dma,
            dma,
            dma,
        ],
        compiler_params=pltpu.CompilerParams(collective_id=0, has_side_effects=True),
        name="exchange",
    )(where, record.reshape(PLANE, CH, SPAN))


def left(x, by):
    return pltpu.roll(x, x.shape[1] - by, 1) if by else x


def correlate_kernel(info_ref, rec_ref, next_ref, tmpl_ref, out_ref, phases, taps, product, power):
    lane = lax.broadcasted_iota(jnp.int32, (CH, 128), 1)
    tap = lax.broadcasted_iota(jnp.int32, (CH, SPAN), 1)
    last = info_ref[EVENTS] == 3

    shifted = []
    norms = []
    for j in range(EVENTS):
        wide = pltpu.roll(tmpl_ref[j // 2, j % 2].astype(F32), SPAN - info_ref[j], 1)
        wide = jnp.where(tap < TAPS, wide, 0.0)
        norms.append(jnp.sum(wide * wide, keepdims=True))
        shifted.append(wide)
    for half in range(2):
        for m in range(4):
            for p in range(4):
                tile = jnp.zeros((CH, 128), F32)
                for i in range(4):
                    piece = shifted[4 * half + i][:, 128 * m : 128 * m + 128]
                    tile = jnp.where(lane // SUB == i, left(piece, SUB * (p - i) % 128), tile)
                row = (4 * m + p) * CH
                taps[row : row + CH, 128 * half : 128 * half + 128] = tile.astype(BF16)
    row = lax.broadcasted_iota(jnp.int32, (256, 256), 0)
    col = lax.broadcasted_iota(jnp.int32, (256, 256), 1)
    order = (lax.rem(row, 8) * SUB + lax.div(row, 8) == col).astype(F32).astype(BF16)
    weights = lax.dot_general(
        order, taps[...], (((1,), (1,)), ((), ())), preferred_element_type=F32
    ).astype(BF16)

    def fill(s, here, after):
        power[pl.ds(s, 1), :] = jnp.sum(here * here, axis=0, keepdims=True)
        joined = jnp.concatenate([here, after], axis=1)
        at = pl.multiple_of(s * SPAN, SPAN)
        for p in range(4):
            phases[p * CH : p * CH + CH, pl.ds(at, SPAN)] = left(joined, SUB * p)[:, :SPAN].astype(BF16)

    def halo():
        return jnp.where(last, 0.0, next_ref[...].astype(F32))

    @pl.loop(0, PLANE - 1)
    def _(s):
        fill(s, rec_ref[s].astype(F32), rec_ref[s + 1, :, 0:128].astype(F32))

    fill(PLANE - 1, rec_ref[PLANE - 1].astype(F32), halo()[:, 0:128])
    fill(PLANE, halo(), jnp.zeros((CH, 128), F32))

    double = jnp.concatenate([power[0:PLANE, :], power[1 : PLANE + 1, :]], axis=1)
    sums = {1: double}
    for size in (1, 2, 4, 8, 16, 32, 64, 128):
        sums[2 * size] = sums[size] + left(sums[size], size)
    energy = sums[256][:, :SPAN]
    start = 256
    for size in (128, 64, 32, 16, 4):
        energy = energy + left(sums[size], start)[:, :SPAN]
        start += size

    spread = lax.broadcasted_iota(jnp.int32, (1, 128), 1)
    norm_row = jnp.zeros((1, 128), F32)
    for j in range(EVENTS):
        norm_row = jnp.where(spread == j, norms[j], norm_row)

    for s in range(PLANE):
        for i in range(4):
            out_ref[s, i : i + 1, SPAN:WIDE] = energy[s : s + 1, 128 * i : 128 * i + 128]
        out_ref[s, 4:5, SPAN:WIDE] = norm_row
        out_ref[s, 5:8, SPAN:WIDE] = jnp.zeros((3, 128), F32)

    @pl.loop(0, PLANE * SPAN // CHUNK)
    def _(c):
        at = pl.multiple_of(c * CHUNK, CHUNK)
        stack = jnp.concatenate([phases[:, pl.ds(at + 128 * m, CHUNK + 128)] for m in range(4)], axis=0)
        product[...] = jnp.dot(weights, stack, preferred_element_type=F32)
        total = product[0:8, 0:CHUNK]
        for b in range(1, SUB):
            total = total + left(product[8 * b : 8 * b + 8, :], b)[:, :CHUNK]
        for q in range(CHUNK // SPAN):
            out_ref[c * (CHUNK // SPAN) + q, :, 0:SPAN] = total[:, SPAN * q : SPAN * q + SPAN]


def correlate(info, record, follower, templates):
    return pl.pallas_call(
        correlate_kernel,
        out_shape=jax.ShapeDtypeStruct((PLANE, EVENTS, WIDE), F32),
        in_specs=[pl.BlockSpec(memory_space=pltpu.SMEM)] + [pl.BlockSpec(memory_space=pltpu.VMEM)] * 3,
        out_specs=pl.BlockSpec(memory_space=pltpu.VMEM),
        scratch_shapes=[
            pltpu.VMEM((4 * CH, (PLANE + 1) * SPAN), BF16),
            pltpu.VMEM((SPAN, 256), BF16),
            pltpu.VMEM((256, CHUNK + 128), F32),
            pltpu.VMEM((24, SPAN), F32),
        ],
        name="correlate",
    )(info, record, follower, templates)


def combine_kernel(part_ref, score_ref, arrived, quad, s_xy, r_xy, s_q, r_q):
    me = {a: lax.axis_index(a) for a in AXES}
    greet(me, [("y", "x"), ("zl", "core")])
    here = spot(me, ("y", "x"))
    flat = steps(("y", "x"))
    out = []
    for by in flat:
        to = moved(me, by)
        there = spot(to, ("y", "x"))
        copy = remote(part_ref.at[there], arrived.at[here], s_xy.at[there], r_xy.at[here], to)
        copy.start()
        out.append(copy)
    arrived[here] = part_ref[here]
    for by in flat:
        source = moved(me, by, -1)
        there = spot(source, ("y", "x"))
        remote(part_ref.at[there], arrived.at[there], s_xy.at[there], r_xy.at[there], source).wait_recv()
    mine = spot(me, ("zl", "core"))
    quad[mine] = jnp.sum(arrived[...], axis=0)
    near = steps(("zl", "core"))
    for by in near:
        to = moved(me, by)
        copy = remote(quad.at[mine], quad.at[mine], s_q.at[spot(to, ("zl", "core"))], r_q.at[mine], to)
        copy.start()
        out.append(copy)
    for by in near:
        source = moved(me, by, -1)
        there = spot(source, ("zl", "core"))
        remote(quad.at[there], quad.at[there], s_q.at[there], r_q.at[there], source).wait_recv()
    total = (quad[0] + quad[1]) + (quad[2] + quad[3])
    corner = total[:, SPAN:WIDE]
    energy = jnp.concatenate([corner[i : i + 1, :] for i in range(4)], axis=1)
    row = lax.broadcasted_iota(jnp.int32, (EVENTS, 128), 0)
    col = lax.broadcasted_iota(jnp.int32, (EVENTS, 128), 1)
    norm = jnp.sum(jnp.where(row == col, corner[4:5, :], 0.0), axis=1, keepdims=True)
    score_ref[...] = total[:, 0:SPAN] / jnp.sqrt(energy * norm + 1e-6)
    for copy in out:
        copy.wait_send()


def combine(parts):
    dma = pltpu.SemaphoreType.DMA
    return pl.pallas_call(
        combine_kernel,
        out_shape=jax.ShapeDtypeStruct((EVENTS, SPAN), F32),
        in_specs=[pl.BlockSpec(memory_space=pltpu.VMEM)],
        out_specs=pl.BlockSpec(memory_space=pltpu.VMEM),
        scratch_shapes=[
            pltpu.VMEM((PLANE, EVENTS, WIDE), F32),
            pltpu.VMEM((4, EVENTS, WIDE), F32),
            dma((PLANE,)),
            dma((PLANE,)),
            dma((4,)),
            dma((4,)),
        ],
        compiler_params=pltpu.CompilerParams(collective_id=1, has_side_effects=True),
        name="combine",
    )(parts)


def local(record, event_stretch, event_offset):
    where = event_stretch.reshape(EVENTS)
    plane = lax.axis_index("zh").astype(jnp.int32)
    info = jnp.concatenate([event_offset.reshape(EVENTS), plane[None]])
    taken, follower, templates = exchange(where, record)
    parts = correlate(info, taken, follower, templates)
    return combine(parts).reshape(4, 2, SPAN)


def solution(mesh):
    torus = Mesh(mesh.devices.reshape(4, 4, 4, 2, 2), AXES)
    return jax.shard_map(
        local,
        mesh=torus,
        in_specs=(P(("zl", "core"), ("zh", "y", "x")), P(), P()),
        out_specs=P(None, None, ("zh", "y", "x")),
        check_vma=False,
    )
```

time: 537 us -> 63.1 us (0.12); the launches traced: 526 us -> 62.9 us
  waiting for transfers between devices: 179 us -> 0 us
  local copies, waits for them, and re-layouts: 129 us -> 2.96 us
  starting transfers between devices: 119 us -> 0 us
  Pallas kernels: 0 us -> 59.3 us
  other arithmetic: 38.3 us -> 0.6 us
  blocking collectives: 26.7 us -> 0 us
  between operations: 20.8 us -> 0.02 us
  matrix products: 12.9 us -> 0 us
    all_to_all x19 -> x0, waiting for transfers between devices: 179 us -> none  [the longest x4 86.1 us: sum_at_owner(): blocks = lax.all_to_all(cut_along(x, dim, peers), axis, 0, 0, tiled=True)]
    all_to_all x19 -> x0, starting transfers between devices: 118 us -> none  [the longest x11 65.3 us: copy_for_each(): lax.all_to_all(jnp.broadcast_to(x[None], (peers, *x.shape)), axis, 0, 0,...]
    reshape x13 -> x3, local copies, waits for them, and re-layouts: 76.2 us -> 2.05 us  [the longest x1 1.34 us: local(): return combine(parts).reshape(4, 2, SPAN)]
    pallas_call x0 -> x3, Pallas kernels: none -> 59.3 us  [the longest x1 31.3 us: exchange(): pl.pallas_call(exchange_kernel, out_shape=(jax.ShapeDtypeStruct((PLANE, C...]
    all_to_all x2 -> x0, blocking collectives: 26.7 us -> none  [copy_for_each(): lax.all_to_all(jnp.broadcast_to(x[None], (peers, *x.shape)), axis, 0, 0,...]
    pad x4 -> x0, local copies, waits for them, and re-layouts: 24 us -> none  [diagonal(): flat = jnp.pad(flat, ((0, 0), (0, taps)))]
    reduce_sum x26 -> x0, other arithmetic: 23.9 us -> none  [the longest x4 10.8 us: sum_at_owner(): return jnp.sum(blocks, axis=0)]
    another operation x7 -> x0, other arithmetic: 14.1 us -> none  [the longest x3 13.1 us: local(): jnp.stack(masked).reshape(len(step_list), 2, record.shape[0], TAPS)]
  transfers between devices with their start and end apart: 20 -> 0, of which waited for: 15 -> 0; matrix products, arithmetic and copies ran while one was open for 32% -> 0% of each run, Pallas kernels for 0% -> 0%
where the time goes in v1:
time: 63.1 us; the launch traced here: 62.9 us
  Pallas kernels  59.3 us (94%)
  local copies, waits for them, and re-layouts  2.96 us (5%)
    pallas_call x1, Pallas kernels, exchange(): pl.pallas_call(exchange_kernel, out_shape=(jax.ShapeDtypeStruct((PLANE, C...  31.3 us
    pallas_call x1, Pallas kernels, combine(): pl.pallas_call(combine_kernel, out_shape=jax.ShapeDtypeStruct((EVENTS, SP...  19.3 us
    pallas_call x1, Pallas kernels, correlate(): pl.pallas_call(correlate_kernel, out_shape=jax.ShapeDtypeStruct((PLANE, E...  8.67 us
    reshape x1, local copies, waits for them, and re-layouts, local(): return combine(parts).reshape(4, 2, SPAN)  1.34 us

profile of v1, /device:TPU:1, one launch (start us, length us, event | category | flops | bytes accessed | tf_op | source)
XLA Modules:
  0.0 62.9 jit_solution(6676472706677378821)
XLA Ops:
  0.0 0.0 copy-start
  0.0 0.7 %copy-done = s32[4,2]{0,1:T(2,128)S(1)} copy-done((s32[4,2]{0,1:T(2,128)S(1)}, s32[4,2]{0,1:T(2,128)}, u32[]{:S(2)}) %copy-start) | copy-done | bytes 56
  0.7 0.1 copy.7
  0.8 0.0 copy-start.1
  0.8 0.6 reshape.13.where_ref
  1.4 0.1 copy-done.1
  1.5 0.1 copy.6
  1.5 0.1 reshape.12
  1.6 0.6 pad_add_fusion.info_ref
  2.2 31.3 %exchange.1 = (bf16[16,32,512]{2,1,0:T(8,128)(2,1)}, bf16[32,512]{1,0:T(8,128)(2,1)}, bf16[4,2,32,512]{3,2,1,0:T(8,128)(2,1)}) custom-call(s32[8]{0:T(128)} %reshape.13.where_ref, bf16[16,32,512]{2,1,0:T(8,128)(2,1)} %bitcast.2), custom_call_target="tpu_custom_call" | custom-call | tf_op jit(solution)/shard_map/exchange/pallas_call | solution.py:114
  33.6 8.7 %correlate.1.part_ref = f32[16,8,640]{2,1,0:T(8,128)} custom-call(s32[9]{0:T(128)} %pad_add_fusion.info_ref, bf16[16,32,512]{2,1,0:T(8,128)(2,1)} %get-tuple-element.8.rec_ref, bf16[32,512]{1,0:T(8,128)(2,1)} %get-tuple-element.9.next_ref, bf16[4,2,32,512]{3,2,1,0:T(8,128)(2,1)} %get-tuple-element.10.tmpl_ref), custom_call_target="tpu_custom_call" | custom-call | tf_op jit(solution)/shard_map/correlate/pallas_call | solution.py:224
  42.2 19.3 %combine.1 = f32[8,512]{1,0:T(8,128)} custom-call(f32[16,8,640]{2,1,0:T(8,128)} %correlate.1.part_ref), custom_call_target="tpu_custom_call" | custom-call | tf_op jit(solution)/shard_map/combine/pallas_call | solution.py:281
  61.5 1.3 %reshape.15 = f32[4,2,512]{2,1,0:T(2,128)} reshape(f32[8,512]{1,0:T(8,128)} %combine.1) | data formatting | bytes 32768 | tf_op jit(solution)/shard_map/reshape | solution.py:305
Async XLA Ops:
  0.0 0.7 %copy-start = (s32[4,2]{0,1:T(2,128)S(1)}, s32[4,2]{0,1:T(2,128)}, u32[]{:S(2)}) copy-start(s32[4,2]{0,1:T(2,128)} %param.4) | copy-start | bytes 100
  0.8 0.7 %copy-start.1 = (s32[4,2]{0,1:T(2,128)S(1)}, s32[4,2]{0,1:T(2,128)}, u32[]{:S(2)}) copy-start(s32[4,2]{0,1:T(2,128)} %param.5) | copy-start | bytes 100

commit v2 on v1

v2 whole, which is shorter than its diff:
```python
import functools
import itertools

import jax
import jax.numpy as jnp
from jax import lax
from jax.experimental import pallas as pl
from jax.experimental.pallas import tpu as pltpu
from jax.sharding import Mesh
from jax.sharding import PartitionSpec as P

TAPS = 500
AXES = ("zh", "y", "x", "zl", "core")
SIZE = {"zh": 4, "y": 4, "x": 4, "zl": 2, "core": 2}
MESH = pl.DeviceIdType.MESH
F32 = jnp.float32
BF16 = jnp.bfloat16
SPAN = 512
PLANE = 16
CH = 32
HALF = 16
EVENTS = 8
SUB = 32
CHUNK = 2048
WIDE = SPAN + 128


def steps(axes):
    grid = itertools.product(*[range(SIZE[a]) for a in axes])
    return [dict(zip(axes, at)) for at in grid if any(at)]


def moved(me, by, sign=1):
    return {a: lax.rem(me[a] + sign * by[a] + SIZE[a], SIZE[a]) for a in by}


def spot(at, axes):
    index = 0
    for a in axes:
        index = index * SIZE[a] + at[a]
    return index


def remote(src, dst, send, recv, to):
    return pltpu.make_async_remote_copy(
        src_ref=src, dst_ref=dst, send_sem=send, recv_sem=recv, device_id=to, device_id_type=MESH
    )


def greet(me, groups):
    barrier = pltpu.get_barrier_semaphore()
    count = 0
    for axes in groups:
        for by in steps(axes):
            pl.semaphore_signal(barrier, inc=1, device_id=moved(me, by), device_id_type=MESH)
            count += 1
    pl.semaphore_wait(barrier, count)


def left(x, by):
    return pltpu.roll(x, x.shape[1] - by, 1) if by else x


def kernel(
    stretch_ref,
    offset_ref,
    x_ref,
    score_ref,
    rec0,
    rec1,
    next0,
    next1,
    cand0,
    cand1,
    picks0,
    picks1,
    tmpl0,
    tmpl1,
    phases,
    taps,
    product0,
    product1,
    power,
    part,
    arrived,
    quad,
    s_xy,
    r_xy,
    s_z,
    r_z,
    s_g,
    r_g,
    s_h,
    r_h,
    own,
    s_p,
    r_p,
    s_q,
    r_q,
):
    me = {a: lax.axis_index(a) for a in AXES}
    greet(me, [("y", "x"), ("zh",), ("zl", "core")])
    here = spot(me, ("y", "x"))
    zh = me["zh"]
    flat = steps(("y", "x"))
    recs, nexts, cands, pickss, tmpls = (rec0, rec1), (next0, next1), (cand0, cand1), (picks0, picks1), (tmpl0, tmpl1)
    out = []

    kept = []
    for h in range(2):
        rows = slice(HALF * h, HALF * h + HALF)
        for by in flat:
            to = moved(me, by)
            there = spot(to, ("y", "x"))
            copy = remote(
                x_ref.at[there, rows], recs[h].at[here], s_xy.at[h, there], r_xy.at[h, here], to
            )
            copy.start()
            out.append(copy)
        keep = pltpu.make_async_copy(x_ref.at[here, rows], recs[h].at[here], own.at[h])
        keep.start()
        kept.append(keep)

    back = {"zh": lax.rem(zh + 3, 4)}
    halos = []
    for h in range(2):
        rows = slice(HALF * h, HALF * h + HALF)
        kept[h].wait()
        for by in flat:
            source = moved(me, by, -1)
            there = spot(source, ("y", "x"))
            remote(
                x_ref.at[there, rows], recs[h].at[there], s_xy.at[h, there], r_xy.at[h, there], source
            ).wait_recv()
        for j in range(EVENTS):
            cands[h][j // 2, j % 2] = recs[h][lax.rem(stretch_ref[j // 2, j % 2], PLANE)]
        for d in (2, 1, 3):
            q = lax.rem(zh + d, 4)
            copy = remote(cands[h].at[q], pickss[h].at[zh], s_z.at[h, q], r_z.at[h, zh], {"zh": q})
            copy.start()
            out.append(copy)
        pickss[h][zh] = cands[h][zh]
    for h in range(2):
        halo = remote(recs[h].at[0], nexts[h], s_h.at[h], r_h.at[h], back)
        halo.start()
        halos.append(halo)

    tap = lax.broadcasted_iota(jnp.int32, (HALF, SPAN), 1)
    for h in range(2):
        for d in (1, 2, 3):
            q = lax.rem(zh + d, 4)
            remote(cands[h].at[q], pickss[h].at[q], s_z.at[h, q], r_z.at[h, q], {"zh": q}).wait_recv()
        for i in range(2):
            wide = pickss[h][lax.div(stretch_ref[zh, i], PLANE), i].astype(F32)
            shift = jnp.full((HALF, SPAN), offset_ref[zh, i], jnp.int32)
            for bit in (1, 2, 4, 8):
                wide = jnp.where((shift & bit) != 0, left(wide, bit), wide)
            tmpls[h][zh, i] = jnp.where(tap < TAPS, wide, 0.0).astype(BF16)
        for d in (2, 1, 3):
            q = lax.rem(zh + d, 4)
            copy = remote(tmpls[h].at[zh], tmpls[h].at[zh], s_g.at[h, q], r_g.at[h, zh], {"zh": q})
            copy.start()
            out.append(copy)

    def fill(s, here, after):
        total = None
        at = pl.multiple_of(s * SPAN, SPAN)
        for h in range(2):
            wide = here[h].astype(F32)
            square = jnp.sum(wide * wide, axis=0, keepdims=True)
            total = square if h == 0 else total + square
            joined = jnp.concatenate([here[h], after[h]], axis=1)
            for p in range(4):
                row = p * CH + h * HALF
                phases[row : row + HALF, pl.ds(at, SPAN)] = left(joined, SUB * p)[:, :SPAN]
        power[pl.ds(s, 1), :] = total

    @pl.loop(0, PLANE - 1)
    def _(s):
        fill(s, [r[s] for r in recs], [r[s + 1, :, 0:128] for r in recs])

    for halo in halos:
        halo.wait_recv()
    inside = (zh < 3).astype(F32)
    follow = [(n[...].astype(F32) * inside).astype(BF16) for n in nexts]
    fill(PLANE - 1, [r[PLANE - 1] for r in recs], [f[:, 0:128] for f in follow])
    fill(PLANE, follow, [jnp.zeros((HALF, 128), BF16)] * 2)

    double = jnp.concatenate([power[0:PLANE, :], power[1 : PLANE + 1, :]], axis=1)
    sums = {1: double}
    for size in (1, 2, 4, 8, 16, 32, 64, 128):
        sums[2 * size] = sums[size] + left(sums[size], size)
    energy = sums[256][:, :SPAN]
    start = 256
    for size in (128, 64, 32, 16, 4):
        energy = energy + left(sums[size], start)[:, :SPAN]
        start += size
    for s in range(PLANE):
        for i in range(4):
            part[s, i : i + 1, SPAN:WIDE] = energy[s : s + 1, 128 * i : 128 * i + 128]

    row = lax.broadcasted_iota(jnp.int32, (256, 256), 0)
    col = lax.broadcasted_iota(jnp.int32, (256, 256), 1)
    order = (lax.rem(row, 8) * SUB + lax.div(row, 8) == col).astype(F32).astype(BF16)
    group = lax.div(lax.broadcasted_iota(jnp.int32, (HALF, 128), 1), SUB).astype(F32).astype(BF16)
    for h in range(2):
        for d in (1, 2, 3):
            q = lax.rem(zh + d, 4)
            remote(tmpls[h].at[q], tmpls[h].at[q], s_g.at[h, q], r_g.at[h, q], {"zh": q}).wait_recv()
        for half in range(2):
            for m in range(4):
                pieces = [
                    tmpls[h][(4 * half + i) // 2, i % 2, :, 128 * m : 128 * m + 128] for i in range(4)
                ]
                for p in range(4):
                    tile = left(pieces[0], SUB * p)
                    for i in range(1, 4):
                        tile = jnp.where(group == i, left(pieces[i], SUB * (p - i) % 128), tile)
                    at = (4 * m + p) * CH + HALF * h
                    taps[at : at + HALF, 128 * half : 128 * half + 128] = tile
    weights = lax.dot_general(
        order, taps[...], (((1,), (1,)), ((), ())), preferred_element_type=F32
    ).astype(BF16)

    spread = lax.broadcasted_iota(jnp.int32, (1, 128), 1)
    norms = jnp.zeros((1, 128), F32)
    for j in range(EVENTS):
        both = [t[j // 2, j % 2].astype(F32) for t in tmpls]
        norm = jnp.sum(both[0] * both[0] + both[1] * both[1], keepdims=True)
        norms = jnp.where(spread == j, norm, norms)
    rest = jnp.concatenate([norms, jnp.zeros((3, 128), F32)], axis=0)
    for s in range(PLANE):
        part[s, 4:8, SPAN:WIDE] = rest

    products = (product0, product1)
    turns = [lax.rem(me["y"] + d, 4) for d in (2, 1, 3, 0)]

    def multiply(i):
        at = pl.multiple_of(turns[i] * CHUNK, CHUNK)
        stack = jnp.concatenate([phases[:, pl.ds(at + 128 * m, CHUNK + 128)] for m in range(4)], axis=0)
        products[i % 2][...] = jnp.dot(weights, stack, preferred_element_type=F32)

    multiply(0)
    for i in range(4):
        if i < 3:
            multiply(i + 1)
        product = products[i % 2]
        total = product[0:8, 0:CHUNK]
        for b in range(1, SUB):
            total = total + left(product[8 * b : 8 * b + 8, :], b)[:, :CHUNK]
        for q in range(4):
            part[turns[i] * 4 + q, :, 0:SPAN] = total[:, SPAN * q : SPAN * q + SPAN]
        for dx in (2, 1, 3, 0):
            if i == 3 and dx == 0:
                continue
            to = {"y": turns[i], "x": lax.rem(me["x"] + dx, 4)}
            there = spot(to, ("y", "x"))
            copy = remote(part.at[there], arrived.at[here], s_p.at[there], r_p.at[here], to)
            copy.start()
            out.append(copy)
    arrived[here] = part[here]
    for by in flat:
        source = moved(me, by, -1)
        there = spot(source, ("y", "x"))
        remote(part.at[there], arrived.at[there], s_p.at[there], r_p.at[there], source).wait_recv()

    mine = spot(me, ("zl", "core"))
    quad[mine] = jnp.sum(arrived[...], axis=0)
    near = steps(("zl", "core"))
    for by in near[::-1]:
        to = moved(me, by)
        copy = remote(quad.at[mine], quad.at[mine], s_q.at[spot(to, ("zl", "core"))], r_q.at[mine], to)
        copy.start()
        out.append(copy)
    for by in near:
        source = moved(me, by, -1)
        there = spot(source, ("zl", "core"))
        remote(quad.at[there], quad.at[there], s_q.at[there], r_q.at[there], source).wait_recv()
    total = (quad[0] + quad[1]) + (quad[2] + quad[3])
    corner = total[:, SPAN:WIDE]
    energy = jnp.concatenate([corner[i : i + 1, :] for i in range(4)], axis=1)
    row = lax.broadcasted_iota(jnp.int32, (EVENTS, 128), 0)
    col = lax.broadcasted_iota(jnp.int32, (EVENTS, 128), 1)
    norm = jnp.sum(jnp.where(row == col, corner[4:5, :], 0.0), axis=1, keepdims=True)
    score = total[:, 0:SPAN] / jnp.sqrt(energy * norm + 1e-6)
    for i in range(4):
        score_ref[i] = score[2 * i : 2 * i + 2, :]
    for copy in out:
        copy.wait_send()
    for halo in halos:
        halo.wait_send()


def local(record, event_stretch, event_offset):
    dma = pltpu.SemaphoreType.DMA
    blocks = pltpu.VMEM((PLANE, HALF, SPAN), BF16)
    pairs = pltpu.VMEM((4, 2, HALF, SPAN), BF16)
    return pl.pallas_call(
        kernel,
        out_shape=jax.ShapeDtypeStruct((4, 2, SPAN), F32),
        in_specs=[pl.BlockSpec(memory_space=pltpu.SMEM)] * 2 + [pl.BlockSpec(memory_space=pl.ANY)],
        out_specs=pl.BlockSpec(memory_space=pltpu.VMEM),
        scratch_shapes=[blocks] * 2
        + [pltpu.VMEM((HALF, SPAN), BF16)] * 2
        + [pairs] * 6
        + [
            pltpu.VMEM((4 * CH, (PLANE + 1) * SPAN), BF16),
            pltpu.VMEM((SPAN, 256), BF16),
            pltpu.VMEM((256, CHUNK + 128), F32),
            pltpu.VMEM((256, CHUNK + 128), F32),
            pltpu.VMEM((24, SPAN), F32),
            pltpu.VMEM((PLANE, EVENTS, WIDE), F32),
            pltpu.VMEM((PLANE, EVENTS, WIDE), F32),
            pltpu.VMEM((4, EVENTS, WIDE), F32),
        ]
        + [dma((2, PLANE))] * 2
        + [dma((2, 4))] * 4
        + [dma((2,))] * 3
        + [dma((PLANE,))] * 2
        + [dma((4,))] * 2,
        compiler_params=pltpu.CompilerParams(collective_id=0, has_side_effects=True),
        name="matching",
    )(event_stretch, event_offset, record.reshape(PLANE, CH, SPAN))


def solution(mesh):
    torus = Mesh(mesh.devices.reshape(4, 4, 4, 2, 2), AXES)
    return jax.shard_map(
        local,
        mesh=torus,
        in_specs=(P(("zl", "core"), ("zh", "y", "x")), P(), P()),
        out_specs=P(None, None, ("zh", "y", "x")),
        check_vma=False,
    )
```

time: 63.1 us -> 49.2 us (0.78)
  Pallas kernels: 59.3 us -> 45.5 us
    pallas_call x3 -> x1, Pallas kernels: 59.3 us -> 45.5 us  [local(): pl.pallas_call(kernel, out_shape=jax.ShapeDtypeStruct((4, 2, SPAN), F32),...]
    unnamed x6 -> x7, local copies, waits for them, and re-layouts: 0.92 us -> 3.34 us
    reshape x3 -> x0, local copies, waits for them, and re-layouts: 2.05 us -> none  [the longest x1 1.34 us: local(): return combine(parts).reshape(4, 2, SPAN)]
where the time goes in v2:
time: 49.2 us; the launch traced here: 48.8 us
  Pallas kernels  45.5 us (92%)
  local copies, waits for them, and re-layouts  3.34 us (7%)
    pallas_call x1, Pallas kernels, local(): pl.pallas_call(kernel, out_shape=jax.ShapeDtypeStruct((4, 2, SPAN), F32),...  45.5 us
    unnamed x7, local copies, waits for them, and re-layouts  3.34 us

profile of v2, /device:TPU:1, one launch (start us, length us, event | category | flops | bytes accessed | tf_op | source)
XLA Modules:
  0.0 48.8 jit_solution(14690256923252406767)
XLA Ops:
  0.0 0.0 copy-start
  0.0 0.7 %copy-done = s32[4,2]{0,1:T(2,128)S(1)} copy-done((s32[4,2]{0,1:T(2,128)S(1)}, s32[4,2]{0,1:T(2,128)}, u32[]{:S(2)}) %copy-start) | copy-done | bytes 56
  0.7 0.0 copy-start.1
  0.7 0.7 %copy.4.stretch_ref = s32[4,2]{1,0:T(4,128)} copy(s32[4,2]{0,1:T(2,128)S(1)} %copy-done) | data formatting | bytes 64 | tf_op args[1]
  1.3 0.0 copy-done.1
  1.4 0.7 %copy.5.offset_ref = s32[4,2]{1,0:T(4,128)} copy(s32[4,2]{0,1:T(2,128)S(1)} %copy-done.1) | data formatting | bytes 64 | tf_op args[2]
  2.0 45.5 %matching.1 = f32[4,2,512]{2,1,0:T(2,128)} custom-call(s32[4,2]{1,0:T(4,128)} %copy.4.stretch_ref, s32[4,2]{1,0:T(4,128)} %copy.5.offset_ref, bf16[16,32,512]{2,1,0:T(8,128)(2,1)} %bitcast.1), custom_call_target="tpu_custom_call" | custom-call | tf_op jit(solution)/shard_map/matching/pallas_call | solution.py:298
  47.5 1.3 %copy.7 = f32[4,2,512]{2,1,0:T(2,128)} copy(f32[4,2,512]{2,1,0:T(2,128)} %matching.1) | data formatting | bytes 32768
Async XLA Ops:
  0.0 0.7 %copy-start = (s32[4,2]{0,1:T(2,128)S(1)}, s32[4,2]{0,1:T(2,128)}, u32[]{:S(2)}) copy-start(s32[4,2]{0,1:T(2,128)} %param.4) | copy-start | bytes 100
  0.7 0.7 %copy-start.1 = (s32[4,2]{0,1:T(2,128)S(1)}, s32[4,2]{0,1:T(2,128)}, u32[]{:S(2)}) copy-start(s32[4,2]{0,1:T(2,128)} %param.5) | copy-start | bytes 100

commit v3 on v2

--- a/solution.py
+++ b/solution.py
@@ -22,7 +22,6 @@
 EVENTS = 8
 SUB = 32
 CHUNK = 2048
-WIDE = SPAN + 128
 
 
 def steps(axes):
@@ -84,6 +83,9 @@
     part,
     arrived,
     quad,
+    side,
+    sides,
+    corner,
     s_xy,
     r_xy,
     s_z,
@@ -97,6 +99,10 @@
     r_p,
     s_q,
     r_q,
+    s_e,
+    r_e,
+    s_c,
+    r_c,
 ):
     me = {a: lax.axis_index(a) for a in AXES}
     greet(me, [("y", "x"), ("zh",), ("zl", "core")])
@@ -133,7 +139,7 @@
                 x_ref.at[there, rows], recs[h].at[there], s_xy.at[h, there], r_xy.at[h, there], source
             ).wait_recv()
         for j in range(EVENTS):
-            cands[h][j // 2, j % 2] = recs[h][lax.rem(stretch_ref[j // 2, j % 2], PLANE)]
+            cands[h][j // 2, j % 2] = recs[h][lax.rem(stretch_ref[j % 2, j // 2], PLANE)]
         for d in (2, 1, 3):
             q = lax.rem(zh + d, 4)
             copy = remote(cands[h].at[q], pickss[h].at[zh], s_z.at[h, q], r_z.at[h, zh], {"zh": q})
@@ -151,8 +157,8 @@
             q = lax.rem(zh + d, 4)
             remote(cands[h].at[q], pickss[h].at[q], s_z.at[h, q], r_z.at[h, q], {"zh": q}).wait_recv()
         for i in range(2):
-            wide = pickss[h][lax.div(stretch_ref[zh, i], PLANE), i].astype(F32)
-            shift = jnp.full((HALF, SPAN), offset_ref[zh, i], jnp.int32)
+            wide = pickss[h][lax.div(stretch_ref[i, zh], PLANE), i].astype(F32)
+            shift = jnp.full((HALF, SPAN), offset_ref[i, zh], jnp.int32)
             for bit in (1, 2, 4, 8):
                 wide = jnp.where((shift & bit) != 0, left(wide, bit), wide)
             tmpls[h][zh, i] = jnp.where(tap < TAPS, wide, 0.0).astype(BF16)
@@ -197,7 +203,7 @@
         start += size
     for s in range(PLANE):
         for i in range(4):
-            part[s, i : i + 1, SPAN:WIDE] = energy[s : s + 1, 128 * i : 128 * i + 128]
+            side[s, i : i + 1, :] = energy[s : s + 1, 128 * i : 128 * i + 128]
 
     row = lax.broadcasted_iota(jnp.int32, (256, 256), 0)
     col = lax.broadcasted_iota(jnp.int32, (256, 256), 1)
@@ -230,7 +236,16 @@
         norms = jnp.where(spread == j, norm, norms)
     rest = jnp.concatenate([norms, jnp.zeros((3, 128), F32)], axis=0)
     for s in range(PLANE):
-        part[s, 4:8, SPAN:WIDE] = rest
+        side[s, 4:8, :] = rest
+    for by in flat:
+        to = moved(me, by)
+        there = spot(to, ("y", "x"))
+        copy = remote(side.at[there], sides.at[here], s_e.at[there], r_e.at[here], to)
+        copy.start()
+        out.append(copy)
+    sides[here] = side[here]
+    near = steps(("zl", "core"))
+    mine = spot(me, ("zl", "core"))
 
     products = (product0, product1)
     turns = [lax.rem(me["y"] + d, 4) for d in (2, 1, 3, 0)]
@@ -249,7 +264,7 @@
         for b in range(1, SUB):
             total = total + left(product[8 * b : 8 * b + 8, :], b)[:, :CHUNK]
         for q in range(4):
-            part[turns[i] * 4 + q, :, 0:SPAN] = total[:, SPAN * q : SPAN * q + SPAN]
+            part[turns[i] * 4 + q] = total[:, SPAN * q : SPAN * q + SPAN]
         for dx in (2, 1, 3, 0):
             if i == 3 and dx == 0:
                 continue
@@ -258,15 +273,35 @@
             copy = remote(part.at[there], arrived.at[here], s_p.at[there], r_p.at[here], to)
             copy.start()
             out.append(copy)
+        if i == 2:
+            for by in flat:
+                source = moved(me, by, -1)
+                there = spot(source, ("y", "x"))
+                remote(side.at[there], sides.at[there], s_e.at[there], r_e.at[there], source).wait_recv()
+            corner[mine] = jnp.sum(sides[...], axis=0)
+            for by in near:
+                to = moved(me, by)
+                there = spot(to, ("zl", "core"))
+                copy = remote(corner.at[mine], corner.at[mine], s_c.at[there], r_c.at[mine], to)
+                copy.start()
+                out.append(copy)
+    for by in near:
+        source = moved(me, by, -1)
+        there = spot(source, ("zl", "core"))
+        remote(corner.at[there], corner.at[there], s_c.at[there], r_c.at[there], source).wait_recv()
+    ends = (corner[0] + corner[1]) + (corner[2] + corner[3])
+    energy = jnp.concatenate([ends[i : i + 1, :] for i in range(4)], axis=1)
+    row = lax.broadcasted_iota(jnp.int32, (EVENTS, 128), 0)
+    col = lax.broadcasted_iota(jnp.int32, (EVENTS, 128), 1)
+    norm = jnp.sum(jnp.where(row == col, ends[4:5, :], 0.0), axis=1, keepdims=True)
+    root = jnp.sqrt(energy * norm + 1e-6)
     arrived[here] = part[here]
     for by in flat:
         source = moved(me, by, -1)
         there = spot(source, ("y", "x"))
         remote(part.at[there], arrived.at[there], s_p.at[there], r_p.at[there], source).wait_recv()
 
-    mine = spot(me, ("zl", "core"))
     quad[mine] = jnp.sum(arrived[...], axis=0)
-    near = steps(("zl", "core"))
     for by in near[::-1]:
         to = moved(me, by)
         copy = remote(quad.at[mine], quad.at[mine], s_q.at[spot(to, ("zl", "core"))], r_q.at[mine], to)
@@ -277,12 +312,7 @@
         there = spot(source, ("zl", "core"))
         remote(quad.at[there], quad.at[there], s_q.at[there], r_q.at[there], source).wait_recv()
     total = (quad[0] + quad[1]) + (quad[2] + quad[3])
-    corner = total[:, SPAN:WIDE]
-    energy = jnp.concatenate([corner[i : i + 1, :] for i in range(4)], axis=1)
-    row = lax.broadcasted_iota(jnp.int32, (EVENTS, 128), 0)
-    col = lax.broadcasted_iota(jnp.int32, (EVENTS, 128), 1)
-    norm = jnp.sum(jnp.where(row == col, corner[4:5, :], 0.0), axis=1, keepdims=True)
-    score = total[:, 0:SPAN] / jnp.sqrt(energy * norm + 1e-6)
+    score = total / root
     for i in range(4):
         score_ref[i] = score[2 * i : 2 * i + 2, :]
     for copy in out:
@@ -309,18 +339,20 @@
             pltpu.VMEM((256, CHUNK + 128), F32),
             pltpu.VMEM((256, CHUNK + 128), F32),
             pltpu.VMEM((24, SPAN), F32),
-            pltpu.VMEM((PLANE, EVENTS, WIDE), F32),
-            pltpu.VMEM((PLANE, EVENTS, WIDE), F32),
-            pltpu.VMEM((4, EVENTS, WIDE), F32),
+            pltpu.VMEM((PLANE, EVENTS, SPAN), F32),
+            pltpu.VMEM((PLANE, EVENTS, SPAN), F32),
+            pltpu.VMEM((4, EVENTS, SPAN), F32),
+            pltpu.VMEM((PLANE, EVENTS, 128), F32),
+            pltpu.VMEM((PLANE, EVENTS, 128), F32),
+            pltpu.VMEM((4, EVENTS, 128), F32),
         ]
         + [dma((2, PLANE))] * 2
         + [dma((2, 4))] * 4
         + [dma((2,))] * 3
-        + [dma((PLANE,))] * 2
-        + [dma((4,))] * 2,
+        + [dma((PLANE,)), dma((PLANE,)), dma((4,)), dma((4,))] * 2,
         compiler_params=pltpu.CompilerParams(collective_id=0, has_side_effects=True),
         name="matching",
-    )(event_stretch, event_offset, record.reshape(PLANE, CH, SPAN))
+    )(event_stretch.T, event_offset.T, record.reshape(PLANE, CH, SPAN))
 
 
 def solution(mesh):

time: 49.2 us -> 49.7 us (1.010)
  Pallas kernels: 45.5 us -> 48.1 us
  local copies, waits for them, and re-layouts: 3.34 us -> 1.32 us
    pallas_call x1, Pallas kernels: 45.5 us -> 48.1 us  [local(): pl.pallas_call(kernel, out_shape=jax.ShapeDtypeStruct((4, 2, SPAN), F32),...]
    unnamed x7 -> x1, local copies, waits for them, and re-layouts: 3.34 us -> 1.32 us
where the time goes in v3:
time: 49.7 us; the launch traced here: 49.4 us
  Pallas kernels  48.1 us (97%)
  local copies, waits for them, and re-layouts  1.32 us (3%)
    pallas_call x1, Pallas kernels, local(): pl.pallas_call(kernel, out_shape=jax.ShapeDtypeStruct((4, 2, SPAN), F32),...  48.1 us
    unnamed x1, local copies, waits for them, and re-layouts  1.32 us

profile of v3, /device:TPU:1, one launch (start us, length us, event | category | flops | bytes accessed | tf_op | source)
XLA Modules:
  0.0 49.4 jit_solution(8580101971186476604)
XLA Ops:
  0.0 48.1 %matching.1 = f32[4,2,512]{2,1,0:T(2,128)} custom-call(s32[2,4]{1,0:T(2,128)} %bitcast.4, s32[2,4]{1,0:T(2,128)} %bitcast.5, bf16[16,32,512]{2,1,0:T(8,128)(2,1)} %bitcast.3), custom_call_target="tpu_custom_call" | custom-call | tf_op jit(solution)/shard_map/matching/pallas_call | solution.py:328
  48.1 1.3 %copy.5 = f32[4,2,512]{2,1,0:T(2,128)} copy(f32[4,2,512]{2,1,0:T(2,128)} %matching.1) | data formatting | bytes 32768

commit v4 on v3

v4 whole, which is shorter than its diff:
```python
import functools
import itertools

import jax
import jax.numpy as jnp
from jax import lax
from jax.experimental import pallas as pl
from jax.experimental.pallas import tpu as pltpu
from jax.sharding import Mesh
from jax.sharding import PartitionSpec as P

TAPS = 500
AXES = ("zh", "y", "x", "zl", "core")
SIZE = {"zh": 4, "y": 4, "x": 4, "zl": 2, "core": 2}
MESH = pl.DeviceIdType.MESH
F32 = jnp.float32
BF16 = jnp.bfloat16
SPAN = 512
PLANE = 16
CH = 32
PIECES = 4
ROWS = CH // PIECES
EVENTS = 8
SUB = 32
CHUNK = 2048


def steps(axes):
    grid = itertools.product(*[range(SIZE[a]) for a in axes])
    return [dict(zip(axes, at)) for at in grid if any(at)]


def moved(me, by, sign=1):
    return {a: lax.rem(me[a] + sign * by[a] + SIZE[a], SIZE[a]) for a in by}


def spot(at, axes):
    index = 0
    for a in axes:
        index = index * SIZE[a] + at[a]
    return index


def remote(src, dst, send, recv, to):
    return pltpu.make_async_remote_copy(
        src_ref=src, dst_ref=dst, send_sem=send, recv_sem=recv, device_id=to, device_id_type=MESH
    )


def greet(me, groups):
    barrier = pltpu.get_barrier_semaphore()
    count = 0
    for axes in groups:
        for by in steps(axes):
            pl.semaphore_signal(barrier, inc=1, device_id=moved(me, by), device_id_type=MESH)
            count += 1
    pl.semaphore_wait(barrier, count)


def left(x, by):
    return pltpu.roll(x, x.shape[1] - by, 1) if by else x


def settle(ref, count, send, recv, to):
    whole = remote(ref.at[pl.ds(0, count)], ref.at[pl.ds(0, count)], send, recv, to)
    return whole


def kernel(
    stretch_ref,
    offset_ref,
    x_ref,
    score_ref,
    *scratch,
):
    recs, nexts, cands, pickss, tmpls = (scratch[i * PIECES : i * PIECES + PIECES] for i in range(5))
    (
        phases,
        taps,
        product0,
        product1,
        power,
        part,
        arrived,
        quad,
        side,
        sides,
        corner,
        s_xy,
        r_xy,
        s_z,
        r_z,
        s_g,
        r_g,
        s_h,
        r_h,
        own,
        s_p,
        r_p,
        s_q,
        r_q,
        s_e,
        r_e,
        s_c,
        r_c,
    ) = scratch[5 * PIECES :]
    me = {a: lax.axis_index(a) for a in AXES}
    greet(me, [("y", "x"), ("zh",), ("zl", "core")])
    here = spot(me, ("y", "x"))
    zh = me["zh"]
    flat = steps(("y", "x"))
    beside = moved(me, flat[0])
    above = {"zh": lax.rem(zh + 1, 4)}

    kept = []
    for h in range(PIECES):
        rows = slice(ROWS * h, ROWS * h + ROWS)
        for by in flat:
            to = moved(me, by)
            there = spot(to, ("y", "x"))
            remote(x_ref.at[there, rows], recs[h].at[here], s_xy.at[h], r_xy.at[h], to).start()
        keep = pltpu.make_async_copy(x_ref.at[here, rows], recs[h].at[here], own.at[h])
        keep.start()
        kept.append(keep)

    def pick(h):
        settle(pickss[h], 3, s_z.at[h], r_z.at[h], above).wait_recv()
        for i in range(2):
            wide = pickss[h][lax.div(stretch_ref[i, zh], PLANE), i].astype(F32)
            shift = jnp.full((ROWS, SPAN), offset_ref[i, zh], jnp.int32)
            for bit in (1, 2, 4, 8):
                wide = jnp.where((shift & bit) != 0, left(wide, bit), wide)
            tmpls[h][zh, i] = jnp.where(tap < TAPS, wide, 0.0).astype(BF16)
        for d in (2, 1, 3):
            q = lax.rem(zh + d, 4)
            remote(tmpls[h].at[zh], tmpls[h].at[zh], s_g.at[h], r_g.at[h], {"zh": q}).start()

    back = {"zh": lax.rem(zh + 3, 4)}
    tap = lax.broadcasted_iota(jnp.int32, (ROWS, SPAN), 1)
    halos = []
    for h in range(PIECES):
        rows = slice(ROWS * h, ROWS * h + ROWS)
        kept[h].wait()
        settle(recs[h], PLANE - 1, s_xy.at[h], r_xy.at[h], beside).wait_recv()
        for j in range(EVENTS):
            cands[h][j // 2, j % 2] = recs[h][lax.rem(stretch_ref[j % 2, j // 2], PLANE)]
        for d in (2, 1, 3):
            q = lax.rem(zh + d, 4)
            remote(cands[h].at[q], pickss[h].at[zh], s_z.at[h], r_z.at[h], {"zh": q}).start()
        pickss[h][zh] = cands[h][zh]
        if h >= 2:
            pick(h - 2)
    for h in range(PIECES - 2, PIECES):
        pick(h)
    for h in range(PIECES):
        halo = remote(recs[h].at[0], nexts[h], s_h.at[h], r_h.at[h], back)
        halo.start()
        halos.append(halo)

    def merged(blocks):
        if PIECES == 2:
            return blocks
        return [jnp.concatenate(blocks[i : i + 2], axis=0) for i in (0, 2)]

    def fill(s, here, after):
        total = None
        at = pl.multiple_of(s * SPAN, SPAN)
        here, after = merged(here), merged(after)
        for h in range(2):
            wide = here[h].astype(F32)
            square = jnp.sum(wide * wide, axis=0, keepdims=True)
            total = square if h == 0 else total + square
            joined = jnp.concatenate([here[h], after[h]], axis=1)
            for p in range(4):
                row = p * CH + h * 16
                phases[row : row + 16, pl.ds(at, SPAN)] = left(joined, SUB * p)[:, :SPAN]
        power[pl.ds(s, 1), :] = total

    @pl.loop(0, PLANE - 1)
    def _(s):
        fill(s, [r[s] for r in recs], [r[s + 1, :, 0:128] for r in recs])

    for halo in halos:
        halo.wait_recv()
    inside = (zh < 3).astype(F32)
    follow = [(n[...].astype(F32) * inside).astype(BF16) for n in nexts]
    fill(PLANE - 1, [r[PLANE - 1] for r in recs], [f[:, 0:128] for f in follow])
    fill(PLANE, follow, [jnp.zeros((ROWS, 128), BF16)] * PIECES)
    for h in range(PIECES):
        settle(recs[h], PLANE - 1, s_xy.at[h], r_xy.at[h], beside).wait_send()
        settle(pickss[h], 3, s_z.at[h], r_z.at[h], above).wait_send()

    double = jnp.concatenate([power[0:PLANE, :], power[1 : PLANE + 1, :]], axis=1)
    sums = {1: double}
    for size in (1, 2, 4, 8, 16, 32, 64, 128):
        sums[2 * size] = sums[size] + left(sums[size], size)
    energy = sums[256][:, :SPAN]
    start = 256
    for size in (128, 64, 32, 16, 4):
        energy = energy + left(sums[size], start)[:, :SPAN]
        start += size
    for s in range(PLANE):
        for i in range(4):
            side[s, i : i + 1, :] = energy[s : s + 1, 128 * i : 128 * i + 128]

    row = lax.broadcasted_iota(jnp.int32, (256, 256), 0)
    col = lax.broadcasted_iota(jnp.int32, (256, 256), 1)
    order = (lax.rem(row, 8) * SUB + lax.div(row, 8) == col).astype(F32).astype(BF16)
    group = lax.div(lax.broadcasted_iota(jnp.int32, (16, 128), 1), SUB).astype(F32).astype(BF16)
    for h in range(PIECES):
        settle(tmpls[h], 3, s_g.at[h], r_g.at[h], above).wait_recv()
    for h in range(2):
        for half in range(2):
            for m in range(4):
                pieces = [
                    merged([t[(4 * half + i) // 2, i % 2, :, 128 * m : 128 * m + 128] for t in tmpls])[h]
                    for i in range(4)
                ]
                for p in range(4):
                    tile = left(pieces[0], SUB * p)
                    for i in range(1, 4):
                        tile = jnp.where(group == i, left(pieces[i], SUB * (p - i) % 128), tile)
                    at = (4 * m + p) * CH + 16 * h
                    taps[at : at + 16, 128 * half : 128 * half + 128] = tile
    weights = lax.dot_general(
        order, taps[...], (((1,), (1,)), ((), ())), preferred_element_type=F32
    ).astype(BF16)

    spread = lax.broadcasted_iota(jnp.int32, (1, 128), 1)
    norms = jnp.zeros((1, 128), F32)
    for j in range(EVENTS):
        both = [t[j // 2, j % 2].astype(F32) for t in tmpls]
        norm = jnp.sum(sum(b * b for b in both), keepdims=True)
        norms = jnp.where(spread == j, norm, norms)
    rest = jnp.concatenate([norms, jnp.zeros((3, 128), F32)], axis=0)
    for s in range(PLANE):
        side[s, 4:8, :] = rest
    for by in flat:
        to = moved(me, by)
        there = spot(to, ("y", "x"))
        remote(side.at[there], sides.at[here], s_e, r_e, to).start()
    sides[here] = side[here]
    near = steps(("zl", "core"))
    mine = spot(me, ("zl", "core"))

    products = (product0, product1)
    turns = [lax.rem(me["y"] + d, 4) for d in (2, 1, 3, 0)]

    def multiply(i):
        at = pl.multiple_of(turns[i] * CHUNK, CHUNK)
        stack = jnp.concatenate([phases[:, pl.ds(at + 128 * m, CHUNK + 128)] for m in range(4)], axis=0)
        products[i % 2][...] = jnp.dot(weights, stack, preferred_element_type=F32)

    multiply(0)
    for i in range(4):
        if i < 3:
            multiply(i + 1)
        product = products[i % 2]
        total = product[0:8, 0:CHUNK]
        for b in range(1, SUB):
            total = total + left(product[8 * b : 8 * b + 8, :], b)[:, :CHUNK]
        for q in range(4):
            part[turns[i] * 4 + q] = total[:, SPAN * q : SPAN * q + SPAN]
        for dx in (2, 1, 3, 0):
            if i == 3 and dx == 0:
                continue
            to = {"y": turns[i], "x": lax.rem(me["x"] + dx, 4)}
            there = spot(to, ("y", "x"))
            remote(part.at[there], arrived.at[here], s_p, r_p, to).start()
    settle(sides, PLANE - 1, s_e, r_e, beside).wait_recv()
    corner[mine] = jnp.sum(sides[...], axis=0)
    for by in near:
        remote(corner.at[mine], corner.at[mine], s_c, r_c, moved(me, by)).start()
    arrived[here] = part[here]
    settle(arrived, PLANE - 1, s_p, r_p, beside).wait_recv()

    quad[mine] = jnp.sum(arrived[...], axis=0)
    for by in near[::-1]:
        remote(quad.at[mine], quad.at[mine], s_q, r_q, moved(me, by)).start()
    partner = moved(me, near[0])
    settle(corner, 3, s_c, r_c, partner).wait_recv()
    ends = (corner[0] + corner[1]) + (corner[2] + corner[3])
    energy = jnp.concatenate([ends[i : i + 1, :] for i in range(4)], axis=1)
    row = lax.broadcasted_iota(jnp.int32, (EVENTS, 128), 0)
    col = lax.broadcasted_iota(jnp.int32, (EVENTS, 128), 1)
    norm = jnp.sum(jnp.where(row == col, ends[4:5, :], 0.0), axis=1, keepdims=True)
    root = jnp.sqrt(energy * norm + 1e-6)
    settle(sides, PLANE - 1, s_e, r_e, beside).wait_send()
    settle(arrived, PLANE - 1, s_p, r_p, beside).wait_send()
    settle(corner, 3, s_c, r_c, partner).wait_send()
    for h in range(PIECES):
        settle(tmpls[h], 3, s_g.at[h], r_g.at[h], above).wait_send()
        halos[h].wait_send()
    settle(quad, 3, s_q, r_q, partner).wait_recv()
    total = (quad[0] + quad[1]) + (quad[2] + quad[3])
    score = total / root
    for i in range(4):
        score_ref[i] = score[2 * i : 2 * i + 2, :]
    settle(quad, 3, s_q, r_q, partner).wait_send()


def local(record, event_stretch, event_offset):
    dma = pltpu.SemaphoreType.DMA
    blocks = pltpu.VMEM((PLANE, ROWS, SPAN), BF16)
    pairs = pltpu.VMEM((4, 2, ROWS, SPAN), BF16)
    return pl.pallas_call(
        kernel,
        out_shape=jax.ShapeDtypeStruct((4, 2, SPAN), F32),
        in_specs=[pl.BlockSpec(memory_space=pltpu.SMEM)] * 2 + [pl.BlockSpec(memory_space=pl.ANY)],
        out_specs=pl.BlockSpec(memory_space=pltpu.VMEM),
        scratch_shapes=[blocks] * PIECES
        + [pltpu.VMEM((ROWS, SPAN), BF16)] * PIECES
        + [pairs] * (3 * PIECES)
        + [
            pltpu.VMEM((4 * CH, (PLANE + 1) * SPAN), BF16),
            pltpu.VMEM((SPAN, 256), BF16),
            pltpu.VMEM((256, CHUNK + 128), F32),
            pltpu.VMEM((256, CHUNK + 128), F32),
            pltpu.VMEM((24, SPAN), F32),
            pltpu.VMEM((PLANE, EVENTS, SPAN), F32),
            pltpu.VMEM((PLANE, EVENTS, SPAN), F32),
            pltpu.VMEM((4, EVENTS, SPAN), F32),
            pltpu.VMEM((PLANE, EVENTS, 128), F32),
            pltpu.VMEM((PLANE, EVENTS, 128), F32),
            pltpu.VMEM((4, EVENTS, 128), F32),
        ]
        + [dma((PIECES,))] * 9
        + [dma] * 8,
        compiler_params=pltpu.CompilerParams(collective_id=0, has_side_effects=True),
        name="matching",
    )(event_stretch.T, event_offset.T, record.reshape(PLANE, CH, SPAN))


def solution(mesh):
    torus = Mesh(mesh.devices.reshape(4, 4, 4, 2, 2), AXES)
    return jax.shard_map(
        local,
        mesh=torus,
        in_specs=(P(("zl", "core"), ("zh", "y", "x")), P(), P()),
        out_specs=P(None, None, ("zh", "y", "x")),
        check_vma=False,
    )
```

time: 49.7 us -> 45.8 us (0.922)
  Pallas kernels: 48.1 us -> 44.3 us
    pallas_call x1, Pallas kernels: 48.1 us -> 44.3 us  [local(): pl.pallas_call(kernel, out_shape=jax.ShapeDtypeStruct((4, 2, SPAN), F32),...]
where the time goes in v4:
time: 45.8 us; the launch traced here: 45.6 us
  Pallas kernels  44.3 us (97%)
  local copies, waits for them, and re-layouts  1.32 us (3%)
    pallas_call x1, Pallas kernels, local(): pl.pallas_call(kernel, out_shape=jax.ShapeDtypeStruct((4, 2, SPAN), F32),...  44.3 us
    unnamed x1, local copies, waits for them, and re-layouts  1.32 us

profile of v4, /device:TPU:1, one launch (start us, length us, event | category | flops | bytes accessed | tf_op | source)
XLA Modules:
  0.0 45.6 jit_solution(16269164635440800326)
XLA Ops:
  0.0 44.3 %matching.1 = f32[4,2,512]{2,1,0:T(2,128)} custom-call(s32[2,4]{1,0:T(2,128)} %bitcast.4, s32[2,4]{1,0:T(2,128)} %bitcast.5, bf16[16,32,512]{2,1,0:T(8,128)(2,1)} %bitcast.3), custom_call_target="tpu_custom_call" | custom-call | tf_op jit(solution)/shard_map/matching/pallas_call | solution.py:306
  44.3 1.3 %copy.5 = f32[4,2,512]{2,1,0:T(2,128)} copy(f32[4,2,512]{2,1,0:T(2,128)} %matching.1) | data formatting | bytes 32768

commit v5 on v4

--- a/solution.py
+++ b/solution.py
@@ -67,10 +67,11 @@
 
 
 def kernel(
-    stretch_ref,
-    offset_ref,
+    stretch_hbm,
+    offset_hbm,
     x_ref,
     score_ref,
+    root_ref,
     *scratch,
 ):
     recs, nexts, cands, pickss, tmpls = (scratch[i * PIECES : i * PIECES + PIECES] for i in range(5))
@@ -103,8 +104,17 @@
         r_e,
         s_c,
         r_c,
+        stretch_ref,
+        offset_ref,
+        r_i,
     ) = scratch[5 * PIECES :]
     me = {a: lax.axis_index(a) for a in AXES}
+    tables = [
+        pltpu.make_async_copy(stretch_hbm, stretch_ref, r_i.at[0]),
+        pltpu.make_async_copy(offset_hbm, offset_ref, r_i.at[1]),
+    ]
+    for table in tables:
+        table.start()
     greet(me, [("y", "x"), ("zh",), ("zl", "core")])
     here = spot(me, ("y", "x"))
     zh = me["zh"]
@@ -122,6 +132,9 @@
         keep = pltpu.make_async_copy(x_ref.at[here, rows], recs[h].at[here], own.at[h])
         keep.start()
         kept.append(keep)
+
+    for table in tables:
+        table.wait()
 
     def pick(h):
         settle(pickss[h], 3, s_z.at[h], r_z.at[h], above).wait_recv()
@@ -293,9 +306,9 @@
         halos[h].wait_send()
     settle(quad, 3, s_q, r_q, partner).wait_recv()
     total = (quad[0] + quad[1]) + (quad[2] + quad[3])
-    score = total / root
     for i in range(4):
-        score_ref[i] = score[2 * i : 2 * i + 2, :]
+        score_ref[i] = total[2 * i : 2 * i + 2, :]
+        root_ref[i] = root[2 * i : 2 * i + 2, :]
     settle(quad, 3, s_q, r_q, partner).wait_send()
 
 
@@ -303,11 +316,11 @@
     dma = pltpu.SemaphoreType.DMA
     blocks = pltpu.VMEM((PLANE, ROWS, SPAN), BF16)
     pairs = pltpu.VMEM((4, 2, ROWS, SPAN), BF16)
-    return pl.pallas_call(
+    total, root = pl.pallas_call(
         kernel,
-        out_shape=jax.ShapeDtypeStruct((4, 2, SPAN), F32),
-        in_specs=[pl.BlockSpec(memory_space=pltpu.SMEM)] * 2 + [pl.BlockSpec(memory_space=pl.ANY)],
-        out_specs=pl.BlockSpec(memory_space=pltpu.VMEM),
+        out_shape=(jax.ShapeDtypeStruct((4, 2, SPAN), F32),) * 2,
+        in_specs=[pl.BlockSpec(memory_space=pltpu.HBM)] * 3,
+        out_specs=(pl.BlockSpec(memory_space=pltpu.VMEM),) * 2,
         scratch_shapes=[blocks] * PIECES
         + [pltpu.VMEM((ROWS, SPAN), BF16)] * PIECES
         + [pairs] * (3 * PIECES)
@@ -325,10 +338,13 @@
             pltpu.VMEM((4, EVENTS, 128), F32),
         ]
         + [dma((PIECES,))] * 9
-        + [dma] * 8,
-        compiler_params=pltpu.CompilerParams(collective_id=0, has_side_effects=True),
+        + [dma] * 8
+        + [pltpu.SMEM((2, 4), jnp.int32)] * 2
+        + [dma((2,))],
+        compiler_params=pltpu.CompilerParams(vmem_limit_bytes=56377244, collective_id=0, has_side_effects=True),
         name="matching",
     )(event_stretch.T, event_offset.T, record.reshape(PLANE, CH, SPAN))
+    return total / root
 
 
 def solution(mesh):

time: 45.8 us -> 44.3 us (0.967)
  Pallas kernels: 44.3 us -> 42.8 us
  local copies, waits for them, and re-layouts: 1.32 us -> 0.69 us
  other arithmetic: 0 us -> 0.62 us
    pallas_call x1, Pallas kernels: 44.3 us -> 42.8 us  [local(): pl.pallas_call(kernel, out_shape=(jax.ShapeDtypeStruct((4, 2, SPAN), F32)...]
    unnamed x1 -> x4, local copies, waits for them, and re-layouts: 1.32 us -> 0.69 us
    div x0 -> x1, other arithmetic: none -> 0.62 us  [local(): return total / root]
where the time goes in v5:
time: 44.3 us; the launch traced here: 44.2 us
  Pallas kernels  42.8 us (97%)
  local copies, waits for them, and re-layouts  0.69 us (2%)
  other arithmetic  0.62 us (1%)
    pallas_call x1, Pallas kernels, local(): pl.pallas_call(kernel, out_shape=(jax.ShapeDtypeStruct((4, 2, SPAN), F32)...  42.8 us

profile of v5, /device:TPU:1, one launch (start us, length us, event | category | flops | bytes accessed | tf_op | source)
XLA Modules:
  0.0 44.2 jit_solution(12218885959026278557)
XLA Ops:
  0.0 0.0 copy-start.1
  0.0 0.0 copy-start
  0.0 0.7 %copy-done.1 = s32[4,2]{0,1:T(2,128)S(1)} copy-done((s32[4,2]{0,1:T(2,128)S(1)}, s32[4,2]{0,1:T(2,128)}, u32[]{:S(2)}) %copy-start.1) | copy-done | bytes 56
  0.7 0.0 copy-done
  0.7 42.8 %matching.1 = (f32[4,2,512]{2,1,0:T(2,128)S(1)}, f32[4,2,512]{2,1,0:T(2,128)S(1)}) custom-call(s32[2,4]{1,0:T(2,128)S(1)} %bitcast.3, s32[2,4]{1,0:T(2,128)S(1)} %bitcast.4, bf16[16,32,512]{2,1,0:T(8,128)(2,1)} %bitcast.5), custom_call_target="tpu_custom_call" | custom-call | tf_op jit(solution)/shard_map/matching/pallas_call | solution.py:319
  43.5 0.6 %div.3 = f32[4,2,512]{2,1,0:T(2,128)} divide(f32[4,2,512]{2,1,0:T(2,128)S(1)} %get-tuple-element.7, f32[4,2,512]{2,1,0:T(2,128)S(1)} %get-tuple-element.8) | non-fusion elementwise | flops 4096 | bytes 49152 | tf_op jit(solution)/shard_map/div | solution.py:347
Async XLA Ops:
  0.0 0.7 %copy-start.1 = (s32[4,2]{0,1:T(2,128)S(1)}, s32[4,2]{0,1:T(2,128)}, u32[]{:S(2)}) copy-start(s32[4,2]{0,1:T(2,128)} %param.5) | copy-start | bytes 100
  0.0 0.7 %copy-start = (s32[4,2]{0,1:T(2,128)S(1)}, s32[4,2]{0,1:T(2,128)}, u32[]{:S(2)}) copy-start(s32[4,2]{0,1:T(2,128)} %param.4) | copy-start | bytes 100

commit v6 on v5

--- a/solution.py
+++ b/solution.py
@@ -69,7 +69,7 @@
 def kernel(
     stretch_hbm,
     offset_hbm,
-    x_ref,
+    x_hbm,
     score_ref,
     root_ref,
     *scratch,
@@ -107,15 +107,20 @@
         stretch_ref,
         offset_ref,
         r_i,
+        x_ref,
+        r_x,
     ) = scratch[5 * PIECES :]
     me = {a: lax.axis_index(a) for a in AXES}
     tables = [
         pltpu.make_async_copy(stretch_hbm, stretch_ref, r_i.at[0]),
         pltpu.make_async_copy(offset_hbm, offset_ref, r_i.at[1]),
     ]
+    whole = pltpu.make_async_copy(x_hbm, x_ref, r_x)
+    whole.start()
     for table in tables:
         table.start()
     greet(me, [("y", "x"), ("zh",), ("zl", "core")])
+    whole.wait()
     here = spot(me, ("y", "x"))
     zh = me["zh"]
     flat = steps(("y", "x"))
@@ -161,9 +166,7 @@
             q = lax.rem(zh + d, 4)
             remote(cands[h].at[q], pickss[h].at[zh], s_z.at[h], r_z.at[h], {"zh": q}).start()
         pickss[h][zh] = cands[h][zh]
-        if h >= 2:
-            pick(h - 2)
-    for h in range(PIECES - 2, PIECES):
+    for h in range(PIECES):
         pick(h)
     for h in range(PIECES):
         halo = remote(recs[h].at[0], nexts[h], s_h.at[h], r_h.at[h], back)
@@ -220,13 +223,19 @@
     col = lax.broadcasted_iota(jnp.int32, (256, 256), 1)
     order = (lax.rem(row, 8) * SUB + lax.div(row, 8) == col).astype(F32).astype(BF16)
     group = lax.div(lax.broadcasted_iota(jnp.int32, (16, 128), 1), SUB).astype(F32).astype(BF16)
-    for h in range(PIECES):
-        settle(tmpls[h], 3, s_g.at[h], r_g.at[h], above).wait_recv()
     for h in range(2):
+        for k in range(h * PIECES // 2, (h + 1) * PIECES // 2):
+            settle(tmpls[k], 3, s_g.at[k], r_g.at[k], above).wait_recv()
         for half in range(2):
             for m in range(4):
                 pieces = [
-                    merged([t[(4 * half + i) // 2, i % 2, :, 128 * m : 128 * m + 128] for t in tmpls])[h]
+                    jnp.concatenate(
+                        [
+                            t[(4 * half + i) // 2, i % 2, :, 128 * m : 128 * m + 128]
+                            for t in tmpls[h * PIECES // 2 : (h + 1) * PIECES // 2]
+                        ],
+                        axis=0,
+                    )
                     for i in range(4)
                 ]
                 for p in range(4):
@@ -239,20 +248,22 @@
         order, taps[...], (((1,), (1,)), ((), ())), preferred_element_type=F32
     ).astype(BF16)
 
-    spread = lax.broadcasted_iota(jnp.int32, (1, 128), 1)
-    norms = jnp.zeros((1, 128), F32)
-    for j in range(EVENTS):
-        both = [t[j // 2, j % 2].astype(F32) for t in tmpls]
-        norm = jnp.sum(sum(b * b for b in both), keepdims=True)
-        norms = jnp.where(spread == j, norm, norms)
-    rest = jnp.concatenate([norms, jnp.zeros((3, 128), F32)], axis=0)
-    for s in range(PLANE):
-        side[s, 4:8, :] = rest
-    for by in flat:
-        to = moved(me, by)
-        there = spot(to, ("y", "x"))
-        remote(side.at[there], sides.at[here], s_e, r_e, to).start()
-    sides[here] = side[here]
+    def tell():
+        spread = lax.broadcasted_iota(jnp.int32, (1, 128), 1)
+        norms = jnp.zeros((1, 128), F32)
+        for j in range(EVENTS):
+            both = [t[j // 2, j % 2].astype(F32) for t in tmpls]
+            norm = jnp.sum(sum(b * b for b in both), keepdims=True)
+            norms = jnp.where(spread == j, norm, norms)
+        rest = jnp.concatenate([norms, jnp.zeros((3, 128), F32)], axis=0)
+        for s in range(PLANE):
+            side[s, 4:8, :] = rest
+        for by in flat:
+            to = moved(me, by)
+            there = spot(to, ("y", "x"))
+            remote(side.at[there], sides.at[here], s_e, r_e, to).start()
+        sides[here] = side[here]
+
     near = steps(("zl", "core"))
     mine = spot(me, ("zl", "core"))
 
@@ -280,6 +291,8 @@
             to = {"y": turns[i], "x": lax.rem(me["x"] + dx, 4)}
             there = spot(to, ("y", "x"))
             remote(part.at[there], arrived.at[here], s_p, r_p, to).start()
+        if i == 0:
+            tell()
     settle(sides, PLANE - 1, s_e, r_e, beside).wait_recv()
     corner[mine] = jnp.sum(sides[...], axis=0)
     for by in near:
@@ -340,7 +353,7 @@
         + [dma((PIECES,))] * 9
         + [dma] * 8
         + [pltpu.SMEM((2, 4), jnp.int32)] * 2
-        + [dma((2,))],
+        + [dma((2,)), pltpu.VMEM((PLANE, CH, SPAN), BF16), dma],
         compiler_params=pltpu.CompilerParams(vmem_limit_bytes=56377244, collective_id=0, has_side_effects=True),
         name="matching",
     )(event_stretch.T, event_offset.T, record.reshape(PLANE, CH, SPAN))

time: 44.3 us -> 43.1 us (0.973)
  Pallas kernels: 42.8 us -> 41.6 us
    pallas_call x1, Pallas kernels: 42.8 us -> 41.6 us  [local(): pl.pallas_call(kernel, out_shape=(jax.ShapeDtypeStruct((4, 2, SPAN), F32)...]
where the time goes in v6:
time: 43.1 us; the launch traced here: 43 us
  Pallas kernels  41.6 us (97%)
  local copies, waits for them, and re-layouts  0.69 us (2%)
  other arithmetic  0.62 us (1%)
    pallas_call x1, Pallas kernels, local(): pl.pallas_call(kernel, out_shape=(jax.ShapeDtypeStruct((4, 2, SPAN), F32)...  41.6 us

profile of v6, /device:TPU:1, one launch (start us, length us, event | category | flops | bytes accessed | tf_op | source)
XLA Modules:
  0.0 43.0 jit_solution(9588499208608151895)
XLA Ops:
  0.0 0.0 copy-start.1
  0.0 0.0 copy-start
  0.0 0.7 %copy-done.1 = s32[4,2]{0,1:T(2,128)S(1)} copy-done((s32[4,2]{0,1:T(2,128)S(1)}, s32[4,2]{0,1:T(2,128)}, u32[]{:S(2)}) %copy-start.1) | copy-done | bytes 56
  0.7 0.0 copy-done
  0.7 41.6 %matching.1 = (f32[4,2,512]{2,1,0:T(2,128)S(1)}, f32[4,2,512]{2,1,0:T(2,128)S(1)}) custom-call(s32[2,4]{1,0:T(2,128)S(1)} %bitcast.3, s32[2,4]{1,0:T(2,128)S(1)} %bitcast.4, bf16[16,32,512]{2,1,0:T(8,128)(2,1)} %bitcast.5), custom_call_target="tpu_custom_call" | custom-call | tf_op jit(solution)/shard_map/matching/pallas_call | solution.py:332
  42.3 0.6 %div.3 = f32[4,2,512]{2,1,0:T(2,128)} divide(f32[4,2,512]{2,1,0:T(2,128)S(1)} %get-tuple-element.7, f32[4,2,512]{2,1,0:T(2,128)S(1)} %get-tuple-element.8) | non-fusion elementwise | flops 4096 | bytes 49152 | tf_op jit(solution)/shard_map/div | solution.py:360
Async XLA Ops:
  0.0 0.7 %copy-start.1 = (s32[4,2]{0,1:T(2,128)S(1)}, s32[4,2]{0,1:T(2,128)}, u32[]{:S(2)}) copy-start(s32[4,2]{0,1:T(2,128)} %param.5) | copy-start | bytes 100
  0.0 0.7 %copy-start = (s32[4,2]{0,1:T(2,128)S(1)}, s32[4,2]{0,1:T(2,128)}, u32[]{:S(2)}) copy-start(s32[4,2]{0,1:T(2,128)} %param.4) | copy-start | bytes 100

commit v7 on v6

--- a/solution.py
+++ b/solution.py
@@ -119,7 +119,7 @@
     whole.start()
     for table in tables:
         table.start()
-    greet(me, [("y", "x"), ("zh",), ("zl", "core")])
+    greet(me, [("zh",), ("y", "x"), ("zl", "core")])
     whole.wait()
     here = spot(me, ("y", "x"))
     zh = me["zh"]
@@ -323,6 +323,10 @@
         score_ref[i] = total[2 * i : 2 * i + 2, :]
         root_ref[i] = root[2 * i : 2 * i + 2, :]
     settle(quad, 3, s_q, r_q, partner).wait_send()
+
+
+def pinned(x):
+    return pltpu.with_memory_space_constraint(x, pltpu.HBM)
 
 
 def local(record, event_stretch, event_offset):
@@ -356,7 +360,7 @@
         + [dma((2,)), pltpu.VMEM((PLANE, CH, SPAN), BF16), dma],
         compiler_params=pltpu.CompilerParams(vmem_limit_bytes=56377244, collective_id=0, has_side_effects=True),
         name="matching",
-    )(event_stretch.T, event_offset.T, record.reshape(PLANE, CH, SPAN))
+    )(pinned(event_stretch.T), pinned(event_offset.T), record.reshape(PLANE, CH, SPAN))
     return total / root
 
 

time: 43.1 us -> 42.1 us (0.977)
  local copies, waits for them, and re-layouts: 0.69 us -> 0 us
    unnamed x4 -> x0, local copies, waits for them, and re-layouts: 0.69 us -> none
where the time goes in v7:
time: 42.1 us; the launch traced here: 42 us
  Pallas kernels  41.4 us (98%)
  other arithmetic  0.62 us (1%)
    pallas_call x1, Pallas kernels, local(): pl.pallas_call(kernel, out_shape=(jax.ShapeDtypeStruct((4, 2, SPAN), F32)...  41.4 us

profile of v7, /device:TPU:1, one launch (start us, length us, event | category | flops | bytes accessed | tf_op | source)
XLA Modules:
  0.0 42.0 jit_solution(2579608141318006474)
XLA Ops:
  0.0 41.4 %matching.1 = (f32[4,2,512]{2,1,0:T(2,128)S(1)}, f32[4,2,512]{2,1,0:T(2,128)S(1)}) custom-call(s32[2,4]{1,0:T(2,128)} %bitcast.4, s32[2,4]{1,0:T(2,128)} %bitcast.5, bf16[16,32,512]{2,1,0:T(8,128)(2,1)} %bitcast.3), custom_call_target="tpu_custom_call" | custom-call | tf_op jit(solution)/shard_map/matching/pallas_call | solution.py:336
  41.4 0.6 %div.3 = f32[4,2,512]{2,1,0:T(2,128)} divide(f32[4,2,512]{2,1,0:T(2,128)S(1)} %get-tuple-element.7, f32[4,2,512]{2,1,0:T(2,128)S(1)} %get-tuple-element.8) | non-fusion elementwise | flops 4096 | bytes 49152 | tf_op jit(solution)/shard_map/div | solution.py:364
